TPU v7x, 32 devices: a whole 2x2x4 slice. The times are simulated.
32 devices in a mesh: seq: 16 (over z, y, x), head: 2 (over core).
Axes of the slice: x: 2, y: 2, z: 4, core: 2. Of those that a mesh axis runs over, the one named last changes fastest.
Arguments:
- token_values: bfloat16 [8192, 3072], P('seq', 'head'), may hold values from -6 to 6
- step_logits: bfloat16 [8192, 48], P('seq', 'head'), may hold values from -4 to 8
- write_keys: bfloat16 [8192, 128], P('seq'), may hold values from -6 to 6
- read_queries: bfloat16 [8192, 128], P('seq'), may hold values from -1.5 to 1.5
- target: int32 [8192], P('seq'), may hold values from 0 to 8191, as said below
- doc_lengths: int32 [8], replicated, may hold values from 1 to 4096, 8192 in all
- decay_log: float32 [48], P('head'), may hold values from -12 to 1.4
- step_bias: float32 [48], P('head'), may hold values from -5.5 to -3.5
- skip_gain: float32 [48], P('head'), may hold values from 0.1 to 1.9
- init_state: float32 [48, 64, 128], P('head'), may hold values from -6 to 6
- out_grad: bfloat16 [8192, 3072], P('seq', 'head'), may hold values from -0.59765625 to 0.59765625
Outputs:
- layer_out: bfloat16 [8192, 3072], P('seq', 'head')
- grad_values: bfloat16 [8192, 3072], P('seq', 'head')
- grad_logits: float32 [8192, 48], P('seq', 'head')
- grad_write: float32 [8192, 128], P('seq')
- grad_read: float32 [8192, 128], P('seq')
Inputs may be any that keep to these rules, and one draw needn't show every extreme that they name: target holds every sequence position once. Group the rows by the index of seq that holds them and by target // 512: each group has at most 64 rows, every index of seq sends the same multiset of group sizes and receives the same multiset, and the largest group has exactly 64 rows. `doc_lengths`: the lengths sum to 8192; the longest is exactly 4096.
All inputs are finite; a program needn't handle non-finite values.
Results may differ from a plain program's by a relative error of at most 0.001.
Values may be sent and summed in bfloat16 or wider, within the bound.
No kernel may reach another device: no remote copies, remote signals or barrier semaphores. Data moves between devices by JAX's collectives and lax.ppermute only.
A program may use at most 128 MiB of HBM per device.

v0:
```python
from functools import partial

import jax
import jax.numpy as jnp
from jax import lax
from jax.sharding import PartitionSpec as P

BLOCK = 256


tripled = lax.Precision.HIGH


def entering(value, axis, combine, identity, reverse):
    devices, mine = (lax.axis_size(axis), lax.axis_index(axis))
    everything = jax.tree.map(lambda part: lax.all_gather(part, axis), value)
    start = jax.tree.map(
        lambda part, zero: jnp.broadcast_to(jnp.asarray(zero, part.dtype), part.shape),
        value,
        identity,
    )

    def step(k, before):
        at = devices - 1 - k if reverse else k
        reached = at > mine if reverse else at < mine
        new = combine(before, jax.tree.map(lambda part: part[at], everything))
        return jax.tree.map(lambda a, b: jnp.where(reached, a, b), new, before)

    return lax.fori_loop(0, devices, step, start)


def combine_maps(earlier, later):
    return (earlier[0] * later[0], later[0][:, None, None] * earlier[1] + later[1])


def block_step(carry_state, pieces, decay_rate):
    values_f, step_size, write_f, read_f, reset_int = pieces
    cum_decay = jnp.cumsum(step_size * decay_rate[None, :], axis=0)
    reset_count = jnp.cumsum(reset_int)
    order_pos = jnp.arange(reset_int.shape[0], dtype=jnp.int32)
    causal = (order_pos[:, None] >= order_pos[None, :]) & (
        reset_count[:, None] == reset_count[None, :]
    )
    spread = cum_decay.T[:, :, None] - cum_decay.T[:, None, :]
    within = jnp.exp(jnp.where(causal[None], spread, -jnp.inf))
    scores = jnp.dot(read_f, write_f.T, precision=tripled, preferred_element_type=jnp.float32)
    blend_matrix = scores[None] * within * step_size.T[:, None, :]
    inner_part = jnp.einsum("hts,shp->thp", blend_matrix, values_f, precision=tripled)
    carry_in = jnp.exp(cum_decay) * (reset_count == 0).astype(jnp.float32)[:, None]
    outer_part = (
        jnp.einsum("tn,hpn->thp", read_f, carry_state, precision=tripled) * carry_in[:, :, None]
    )
    last_decay = cum_decay[-1]
    weight = (
        jnp.exp(last_decay[None, :] - cum_decay)
        * (reset_count == reset_count[-1]).astype(jnp.float32)[:, None]
        * step_size
    )
    fresh_state = jnp.einsum("sh,shp,sn->hpn", weight, values_f, write_f, precision=tripled)
    keep_share = jnp.exp(last_decay) * (reset_count[-1] == 0).astype(jnp.float32)
    new_state = keep_share[:, None, None] * carry_state + fresh_state
    return (new_state, inner_part + outer_part)


def local_layer(
    values_f, logits_f, write_f, read_f, start_state, reset_int, decay_log, step_bias, skip_gain
):
    step_size = jax.nn.softplus(logits_f + step_bias[None, :])
    decay_rate = -jnp.exp(decay_log)
    carry_state = start_state
    collected = []
    for index_block in range(values_f.shape[0] // BLOCK):
        lower = index_block * BLOCK
        pieces = (
            values_f[lower : lower + BLOCK],
            step_size[lower : lower + BLOCK],
            write_f[lower : lower + BLOCK],
            read_f[lower : lower + BLOCK],
            reset_int[lower : lower + BLOCK],
        )
        carry_state, block_out = block_step(carry_state, pieces, decay_rate)
        collected.append(block_out)
    ssd_out = jnp.concatenate(collected, axis=0) + skip_gain[None, :, None] * values_f
    return (ssd_out, carry_state)


def body(
    token_values,
    step_logits,
    write_keys,
    read_queries,
    target,
    doc_lengths,
    decay_log,
    step_bias,
    skip_gain,
    init_state,
    out_grad,
):
    rows_per_device = token_values.shape[0]
    seq_count = lax.axis_size("seq")
    heads_dev = decay_log.shape[0]
    head_width = token_values.shape[1] // heads_dev
    state_width = write_keys.shape[1]
    capacity = 2 * rows_per_device // seq_count
    owner_dev = target // rows_per_device
    member_of = (owner_dev[:, None] == jnp.arange(seq_count, dtype=jnp.int32)[None, :]).astype(
        jnp.int32
    )
    earlier_rows = jnp.cumsum(member_of, axis=0) - member_of
    rank_in = jnp.sum(earlier_rows * member_of, axis=1)
    slot_index = owner_dev * capacity + rank_in

    def to_slots(row_data, filler):
        blank_rows = jnp.full((seq_count * capacity,) + row_data.shape[1:], filler, row_data.dtype)
        return (
            blank_rows.at[slot_index]
            .set(row_data)
            .reshape((seq_count, capacity) + row_data.shape[1:])
        )

    both_keys = jnp.concatenate([write_keys, read_queries], axis=1)
    value_slots = to_slots(token_values, 0)
    logit_slots = to_slots(step_logits, 0)
    target_slots = to_slots(target, -1)
    key_slots = to_slots(both_keys, 0)
    got_values, got_logits, got_targets, got_keys = (
        lax.all_to_all(value_slots, "seq", split_axis=0, concat_axis=0, tiled=True),
        lax.all_to_all(logit_slots, "seq", split_axis=0, concat_axis=0, tiled=True),
        lax.all_to_all(target_slots, "seq", split_axis=0, concat_axis=0, tiled=True),
        lax.all_to_all(key_slots, "seq", split_axis=0, concat_axis=0, tiled=True),
    )
    flat_targets = got_targets.reshape(-1)
    place_at = jnp.where(flat_targets >= 0, flat_targets % rows_per_device, rows_per_device)

    def settle(got_data):
        flat_data = got_data.reshape((-1,) + got_data.shape[2:])
        return (
            jnp.zeros((rows_per_device,) + flat_data.shape[1:], flat_data.dtype)
            .at[place_at]
            .set(flat_data, mode="drop")
        )

    values_f = (
        settle(got_values).astype(jnp.float32).reshape(rows_per_device, heads_dev, head_width)
    )
    logits_f = settle(got_logits).astype(jnp.float32)
    placed_keys = settle(got_keys)
    write_f = placed_keys[:, :state_width].astype(jnp.float32)
    read_f = placed_keys[:, state_width:].astype(jnp.float32)
    starts = jnp.cumsum(doc_lengths)[:-1]
    positions = lax.axis_index("seq") * rows_per_device + jnp.arange(
        rows_per_device, dtype=jnp.int32
    )
    reset_int = jnp.any(positions[:, None] == starts[None, :], axis=1).astype(jnp.int32)
    step_size = jax.nn.softplus(logits_f + step_bias[None, :])
    decay_rate = -jnp.exp(decay_log)
    cum_decay = jnp.cumsum(step_size * decay_rate[None, :], axis=0)
    reset_count = jnp.cumsum(reset_int)
    total_decay = cum_decay[-1]
    span_keep = jnp.exp(total_decay) * (reset_count[-1] == 0).astype(jnp.float32)
    tail_weight = (
        jnp.exp(total_decay[None, :] - cum_decay)
        * (reset_count == reset_count[-1]).astype(jnp.float32)[:, None]
        * step_size
    )
    span_state = jnp.einsum("sh,shp,sn->hpn", tail_weight, values_f, write_f, precision=tripled)
    identity_map = (jnp.ones((heads_dev,), jnp.float32), jnp.zeros_like(span_state))
    before_keep, before_state = entering(
        (span_keep, span_state), "seq", combine_maps, identity_map, False
    )
    start_state = before_keep[:, None, None] * init_state + before_state
    layer_fn = partial(
        local_layer,
        reset_int=reset_int,
        decay_log=decay_log,
        step_bias=step_bias,
        skip_gain=skip_gain,
    )
    (ssd_out, end_state), pullback = jax.vjp(
        layer_fn, values_f, logits_f, write_f, read_f, start_state
    )
    incoming_gradient = out_grad.astype(jnp.float32).reshape(rows_per_device, heads_dev, head_width)
    span_grad = pullback((incoming_gradient, jnp.zeros_like(end_state)))[4]
    after_keep, after_grad = entering(
        (span_keep, span_grad), "seq", combine_maps, identity_map, True
    )
    grads = pullback((incoming_gradient, after_grad))
    grad_write, grad_read = lax.psum((grads[2], grads[3]), "head")
    layer_out = ssd_out.reshape(rows_per_device, heads_dev * head_width).astype(jnp.bfloat16)
    grad_values = grads[0].reshape(rows_per_device, heads_dev * head_width).astype(jnp.bfloat16)
    return (layer_out, grad_values, grads[1], grad_write, grad_read)


def solution(mesh):
    return jax.shard_map(
        body,
        mesh=mesh,
        in_specs=(
            P("seq", "head"),
            P("seq", "head"),
            P("seq", None),
            P("seq", None),
            P("seq"),
            P(),
            P("head"),
            P("head"),
            P("head"),
            P("head", None, None),
            P("seq", "head"),
        ),
        out_specs=(
            P("seq", "head"),
            P("seq", "head"),
            P("seq", "head"),
            P("seq", None),
            P("seq", None),
        ),
        check_vma=False,
    )
```

profile of v0, /device:TPU:0, one launch (start us, length us, event | category | flops | bytes accessed | tf_op | source)
XLA Modules:
  0.0 592.6 jit_solution(13412609829575743571)
XLA Ops:
  10.8 2.6 scatter_custom_fusion
  14.1 8.3 %all-to-all-start = ((s32[16,1,64]{2,1,0:T(1,128)}), s32[16,1,64]{2,1,0:T(1,128)S(1)}, u32[]{:S(2)}, u32[]{:S(2)}) async-start(s32[16,1,64]{2,1,0:T(1,128)} %all_to_all.15), calls=%async_computation | async-start | bytes 16384 | tf_op jit(solution)/shard_map/all_to_all | solution.py:130
  27.5 2.9 fusion.161
  31.3 1.8 scatter_custom_fusion.5
  37.1 2.4 copy.266
  39.6 3.1 scatter_custom_fusion.3
  42.8 6.9 %all-to-all-start.3 = ((bf16[16,2,768]{2,1,0:T(2,128)(2,1)}), bf16[16,2,768]{2,1,0:T(2,128)(2,1)S(1)}, u32[]{:S(2)}, u32[]{:S(2)}) async-start(bf16[16,2,768]{2,1,0:T(2,128)(2,1)} %reshape.685), calls=%async_computation.3 | async-start | bytes 98304 | tf_op jit(solution)/shard_map/all_to_all | solution.py:129
  51.0 6.2 %all-to-all-done.3 = bf16[16,2,768]{2,1,0:T(2,128)(2,1)S(1)} async-done(((bf16[16,2,768]{2,1,0:T(2,128)(2,1)}), bf16[16,2,768]{2,1,0:T(2,128)(2,1)S(1)}, u32[]{:S(2)}, u32[]{:S(2)}) %all-to-all-start.3) | async-done | bytes 49184 | tf_op jit(solution)/shard_map/all_to_all | solution.py:129
  57.1 4.2 all-to-all-start.2
  61.7 3.4 scatter_custom_fusion.6
  74.9 5.4 scatter_custom_fusion.4
  80.3 1.5 fusion.69
  81.8 2.6 fusion.71
  84.5 4.9 scatter_custom_fusion.1
  89.4 126.2 %all_to_all.24 = bf16[16,64,1536]{2,1,0:T(8,128)(2,1)} all-to-all(bf16[16,64,1536]{2,1,0:T(8,128)(2,1)S(1)} %bitcast.352), channel_id=1, replica_groups=mesh['seq'=16,'head'=2] {'seq'}, dimensions={0} | all-to-all | bytes 6291456 | tf_op jit(solution)/shard_map/all_to_all | solution.py:128
  215.6 7.4 %scatter_custom_fusion.2 = bf16[512,1536]{1,0:T(8,128)(2,1)S(1)} fusion(s32[1024]{0:T(1024)} %bitcast.383, bf16[1024,1536]{1,0:T(8,128)(2,1)} %bitcast.364, bf16[]{:T(256)} %constant.143.clone.1), kind=kCustom, calls=%fused_computation.115 | custom fusion | bytes 1573376 | tf_op jit(solution)/shard_map/scatter | solution.py:141
  223.0 2.2 copy.258
  225.2 3.9 fusion.29
  229.2 2.2 copy.264
  232.6 2.5 copy.268
  235.1 2.3 copy.267
  241.9 39.1 %all-gather.2 = f32[16,1,24]{2,1,0:T(1,128)S(1)} all-gather(f32[1,1,24]{2,1,0:T(1,128)} %bitcast.386), channel_id=1, replica_groups=mesh['seq'=16,'head'=2] {'seq'}, dimensions={0}, use_global_device_ids=true | all-gather | bytes 1632 | tf_op jit(solution)/shard_map/all_gather | solution.py:16
  284.1 2.3 copy.248
  286.4 2.3 copy.259
  288.7 21.9 %while.33 = (s32[]{:T(128)}, f32[24,64,128]{2,1,0:T(8,128)S(1)}, s32[]{:T(128)}, f32[16,24]{1,0:T(8,128)S(1)}, f32[16,24,64,128]{3,2,1,0:T(8,128)}, /*index=5*/s32[]{:T(128)}, s32[]{:T(128)}, s32[]{:T(128)}, s32[]{:T(128)}) while((s32[]{:T(128)}, f32[24,64,128]{2,1,0:T(8,128)S(1)}, s32[]{:T(128)}, f32[16,24]{1,0:T(8,128)S(1)}, ...), condition=%wide.region_27.28_spmd.clone, body=%wide.region_26.27_spmd.clone.sunk | while | flops 786440 | bytes 2359751 | solution.py:29
  288.7 1.3 fusion.186
  292.8 1.3 fusion.186
  295.5 1.3 fusion.186
  296.9 1.4 fusion.186
  298.3 1.4 fusion.186
  303.9 1.3 fusion.186
  305.2 1.3 fusion.186
  311.2 2.9 fusion.50
  314.1 126.3 %all-gather.6.cloned.1.call-done = f32[384,64,128]{2,1,0:T(8,128)} async-done(((f32[24,64,128]{2,1,0:T(8,128)}), f32[384,64,128]{2,1,0:T(8,128)}) %all-gather.6.cloned.1.call-update) | async-done | bytes 12582928 | tf_op jit(solution)/shard_map/all_gather | solution.py:16
  440.4 40.5 %while.32 = (s32[]{:T(128)}, f32[24]{0:T(128)}, f32[24,64,128]{2,1,0:T(8,128)S(1)}, s32[]{:T(128)}, f32[16,24]{1,0:T(8,128)}, /*index=5*/f32[16,24,64,128]{3,2,1,0:T(8,128)}, s32[]{:T(128)}, s32[]{:T(128)}) while((s32[]{:T(128)}, f32[24]{0:T(128)}, f32[24,64,128]{2,1,0:T(8,128)S(1)}, s32[]{:T(128)}, f32[16,24]{1,0:T(8,128)}, ...), condition=%wide.region_21.22_spmd.clone, body=%wide.region_20.21_spmd.clone.sunk | while | flops 786508 | bytes 2359891 | solution.py:29
  481.0 2.5 multiply_reduce_fusion.4
  483.5 2.3 multiply_reduce_fusion.2
  485.9 2.1 fusion.80
  488.0 1.7 fusion.49
  493.5 1.3 copy.273
  495.7 6.1 %fusion.19 = (f32[24,256]{1,0:T(8,128)S(1)}, f32[24,256]{1,0:T(8,128)S(1)}, f32[24,256]{1,0:T(8,128)}, f32[256,256]{1,0:T(8,128)}) fusion(f32[24,256]{1,0:T(8,128)} %get-tuple-element.384, f32[24,256]{1,0:T(8,128)} %get-tuple-element.387, f32[256,256]{1,0:T(8,128)} %fusion.130, pred[256,256]{1,0:T(8,128)(4,1)} %fusion.97, ...), kind=kOutput, calls=%fused_computation.38 | convolution fusion | flops 221689856 | bytes 2285568 | tf_op jit(solution)/shard_map/transpose(jvp(hts,shp->thp))/dot_general | solution.py:48
  503.2 2.0 fusion.77
  505.3 2.3 multiply_reduce_fusion.3
  507.6 2.0 fusion.76
  510.2 1.3 copy.269
  513.8 6.4 %fusion.17 = (f32[24,256]{1,0:T(8,128)S(1)}, f32[24,256]{1,0:T(8,128)S(1)}, f32[24,256]{1,0:T(8,128)}, f32[256,256]{1,0:T(8,128)S(1)}) fusion(f32[24,256]{1,0:T(8,128)} %get-tuple-element.383, f32[24,256]{1,0:T(8,128)} %get-tuple-element.389, f32[256,256]{1,0:T(8,128)} %fusion.118, pred[256,256]{1,0:T(8,128)(4,1)} %fusion.96, ...), kind=kOutput, calls=%fused_computation.36 | convolution fusion | flops 221689856 | bytes 2285568 | tf_op jit(solution)/shard_map/transpose(jvp(hts,shp->thp))/dot_general | solution.py:48
  520.4 1.4 fusion.75
  525.5 2.5 reduce-window.94
  529.5 2.5 reduce-window.115
  532.7 4.6 bitcast_add_fusion.3
  537.4 2.8 bitcast_add_fusion.2
  540.2 1.9 add_convert_fusion
  542.2 2.8 copy.277
  545.0 5.5 bitcast_add_fusion.5
  550.5 3.1 copy.262
  553.6 5.4 bitcast_add_fusion.4
  559.1 3.2 copy.263
  562.2 1.6 pad_add_fusion
  563.9 1.6 pad_add_fusion.1
  566.4 1.4 fusion.122
  567.9 3.0 fusion.20
  570.9 11.7 %all-reduce.13.cloned.1.call-done = (f32[512,128]{1,0:T(8,128)}, f32[512,128]{1,0:T(8,128)}) async-done(((f32[512,128]{1,0:T(8,128)}, f32[512,128]{1,0:T(8,128)}), (f32[512,128]{1,0:T(8,128)}, f32[512,128]{1,0:T(8,128)})) %all-reduce.13.cloned.1.call-update) | async-done | bytes 524304 | tf_op jit(solution)/shard_map/psum | solution.py:189
  582.5 1.7 copy.355
  584.2 1.7 copy.356
  (343 shorter events, 100.9 us)
Async XLA Ops:
  10.8 28.8 %copy-start.82 = (s32[512]{0:T(512)}, s32[512]{0:T(512)S(1)}, u32[]{:S(2)}) copy-start(s32[512]{0:T(512)S(1)} %compare_select_fusion.7) | copy-start | bytes 6148
  14.1 28.7 %all-to-all-start = ((s32[16,1,64]{2,1,0:T(1,128)}), s32[16,1,64]{2,1,0:T(1,128)S(1)}, u32[]{:S(2)}, u32[]{:S(2)}) async-start(s32[16,1,64]{2,1,0:T(1,128)} %all_to_all.15), calls=%async_computation | async-start | bytes 16384 | tf_op jit(solution)/shard_map/all_to_all | solution.py:130
  26.3 7.7 %copy-start.63 = (s32[256]{0:T(256)}, s32[256]{0:T(256)S(1)}, u32[]{:S(2)}) copy-start(s32[256]{0:T(256)S(1)} %get-tuple-element.368) | copy-start | bytes 3076
  27.5 7.8 %copy-start.65 = (s32[256]{0:T(256)}, s32[256]{0:T(256)S(1)}, u32[]{:S(2)}) copy-start(s32[256]{0:T(256)S(1)} %get-tuple-element.370) | copy-start | bytes 3076
  27.5 3.6 copy-start.52
  30.5 37.8 %copy-start.77 = (f32[24]{0:T(128)}, f32[24]{0:T(128)S(1)}, u32[]{:S(2)}) copy-start(f32[24]{0:T(128)S(1)} %exponential_negate_fusion) | copy-start | bytes 292
  37.1 43.2 %copy-start.1 = (f32[256,1536]{0,1:T(8,128)}, f32[256,1536]{0,1:T(8,128)S(1)}, u32[]{:S(2)}) copy-start(f32[256,1536]{0,1:T(8,128)S(1)} %copy.265) | copy-start | bytes 4718596
  37.1 28.1 %copy-start.76 = (f32[24]{0:T(128)S(1)}, f32[24]{0:T(128)}, u32[]{:S(2)}) copy-start(f32[24]{0:T(128)} %param.22) | copy-start | bytes 292
  39.6 42.2 %copy-start.3 = (f32[256,1536]{0,1:T(8,128)}, f32[256,1536]{0,1:T(8,128)S(1)}, u32[]{:S(2)}) copy-start(f32[256,1536]{0,1:T(8,128)S(1)} %copy.266) | copy-start | bytes 4718596
  42.8 14.4 %all-to-all-start.3 = ((bf16[16,2,768]{2,1,0:T(2,128)(2,1)}), bf16[16,2,768]{2,1,0:T(2,128)(2,1)S(1)}, u32[]{:S(2)}, u32[]{:S(2)}) async-start(bf16[16,2,768]{2,1,0:T(2,128)(2,1)} %reshape.685), calls=%async_computation.3 | async-start | bytes 98304 | tf_op jit(solution)/shard_map/all_to_all | solution.py:129
  51.0 22.3 %copy-start.78 = (s32[1024,1]{0,1:T(1,128)}, s32[1024,1]{0,1:T(1,128)S(1)}, u32[]{:S(2)}) copy-start(s32[1024,1]{0,1:T(1,128)S(1)} %compare_select_fusion.3) | copy-start | bytes 12292
  57.1 17.7 %all-to-all-start.2 = ((bf16[16,64,256]{2,1,0:T(8,128)(2,1)}), bf16[16,64,256]{2,1,0:T(8,128)(2,1)}, u32[]{:S(2)}, u32[]{:S(2)}) async-start(bf16[16,64,256]{2,1,0:T(8,128)(2,1)} %bitcast.365), calls=%async_computation.2 | async-start | bytes 1048576 | tf_op jit(solution)/shard_map/all_to_all | solution.py:131
  61.4 227.3 %all-gather.8.cloned.1.call-start = ((), (), s32[]{:S(2)}) async-start(), calls=%async_computation.5 | async-start | bytes 13369344 | tf_op jit(solution)/shard_map/all_gather | solution.py:16
  65.2 9.7 %copy-start.24 = (bf16[512,24]{0,1:T(8,128)(2,1)}, bf16[512,24]{0,1:T(8,128)(2,1)S(1)}, u32[]{:S(2)}) copy-start(bf16[512,24]{0,1:T(8,128)(2,1)S(1)} %copy.253) | copy-start | bytes 73732
  69.1 4.8 copy-start.46
  70.4 4.5 copy-start.73
  71.2 3.7 copy-start.49
  73.9 411.9 %copy-start.31 = (f32[256,24]{0,1:T(8,128)}, f32[256,24]{0,1:T(8,128)S(1)}, u32[]{:S(2)}) copy-start(f32[256,24]{0,1:T(8,128)S(1)} %exponential_multiply_fusion.1) | copy-start | bytes 73732
  74.7 9.7 %copy-start.28 = (f32[256,24]{0,1:T(8,128)}, f32[256,24]{0,1:T(8,128)S(1)}, u32[]{:S(2)}) copy-start(f32[256,24]{0,1:T(8,128)S(1)} %exponential_multiply_fusion) | copy-start | bytes 73732
  84.4 356.0 %all-gather.6.cloned.1.call-start = ((), (), s32[]{:S(2)}) async-start(), calls=%async_computation.4 | async-start | bytes 13369344 | tf_op jit(solution)/shard_map/all_gather | solution.py:16
  223.0 6.1 %copy-start.5 = (bf16[512,1536]{1,0:T(8,128)(2,1)}, bf16[512,1536]{1,0:T(8,128)(2,1)S(1)}, u32[]{:S(2)}) copy-start(bf16[512,1536]{1,0:T(8,128)(2,1)S(1)} %scatter_custom_fusion.2) | copy-start | bytes 4718596
  225.2 4.0 copy-start
  229.1 353.5 %all-reduce.13.cloned.1.call-start = ((), (), s32[]{:S(2)}) async-start(), calls=%async_computation.6 | async-start | bytes 1048576 | tf_op jit(solution)/shard_map/psum | solution.py:189
  231.3 6.0 %copy-start.80 = (f32[24]{0:T(128)S(1)}, f32[24]{0:T(128)}, u32[]{:S(2)}) copy-start(f32[24]{0:T(128)} %param.23) | copy-start | bytes 292
  231.3 6.8 %copy-start.66 = (s32[256]{0:T(256)S(1)}, s32[256]{0:T(256)}, u32[]{:S(2)}) copy-start(s32[256]{0:T(256)} %copy-done.65) | copy-start | bytes 3076
  231.3 7.9 %copy-start.64 = (s32[256]{0:T(256)S(1)}, s32[256]{0:T(256)}, u32[]{:S(2)}) copy-start(s32[256]{0:T(256)} %copy-done.63) | copy-start | bytes 3076
  232.6 50.2 %copy-start.6 = (bf16[512,1536]{1,0:T(8,128)(2,1)S(1)}, bf16[512,1536]{1,0:T(8,128)(2,1)}, u32[]{:S(2)}) copy-start(bf16[512,1536]{1,0:T(8,128)(2,1)} %copy-done.5) | copy-start | bytes 4718596
  483.5 4.5 copy-start.9
  483.5 4.5 copy-start.13
  483.5 4.5 copy-start.8
  485.9 3.8 copy-start.47
  485.9 3.8 copy-start.50
  485.9 3.8 copy-start.59
  485.9 3.8 copy-start.61
  485.9 3.8 copy-start.69
  485.9 3.8 copy-start.74
  495.7 6.1 %copy-start.38 = (f32[256,24]{0,1:T(8,128)S(1)}, f32[256,24]{0,1:T(8,128)}, u32[]{:S(2)}) copy-start(f32[256,24]{0,1:T(8,128)} %get-tuple-element.401) | copy-start | bytes 73732
  495.7 6.1 %copy-start.48 = (f32[24,2]{0,1:T(2,128)S(1)}, f32[24,2]{0,1:T(2,128)}, u32[]{:S(2)}) copy-start(f32[24,2]{0,1:T(2,128)} %copy-done.46) | copy-start | bytes 580
  495.7 6.1 %copy-start.62 = (f32[256]{0:T(256)S(1)}, f32[256]{0:T(256)}, u32[]{:S(2)}) copy-start(f32[256]{0:T(256)} %compare_convert_fusion.2) | copy-start | bytes 3076
  495.7 6.1 %copy-start.72 = (f32[256]{0:T(256)S(1)}, f32[256]{0:T(256)}, u32[]{:S(2)}) copy-start(f32[256]{0:T(256)} %get-tuple-element.367) | copy-start | bytes 3076
  495.7 6.1 %copy-start.75 = (f32[24]{0:T(128)S(1)}, f32[24]{0:T(128)}, u32[]{:S(2)}) copy-start(f32[24]{0:T(128)} %copy-done.73) | copy-start | bytes 292
  495.7 6.8 %copy-start.10 = (f32[24,64,128]{2,1,0:T(8,128)S(1)}, f32[24,64,128]{2,1,0:T(8,128)}, u32[]{:S(2)}) copy-start(f32[24,64,128]{2,1,0:T(8,128)} %copy-done.9) | copy-start | bytes 2359300
  495.7 6.8 %copy-start.79 = (f32[24]{0:T(128)S(1)}, f32[24]{0:T(128)}, u32[]{:S(2)}) copy-start(f32[24]{0:T(128)} %exponential_multiply_fusion.3) | copy-start | bytes 292
  502.5 5.1 copy-start.33
  503.2 4.4 copy-start.14
  513.7 6.5 %copy-start.39 = (f32[256,24]{0,1:T(8,128)S(1)}, f32[256,24]{0,1:T(8,128)}, u32[]{:S(2)}) copy-start(f32[256,24]{0,1:T(8,128)} %get-tuple-element.403) | copy-start | bytes 73732
  513.7 6.5 %copy-start.51 = (f32[24,2]{0,1:T(2,128)S(1)}, f32[24,2]{0,1:T(2,128)}, u32[]{:S(2)}) copy-start(f32[24,2]{0,1:T(2,128)} %copy-done.49) | copy-start | bytes 580
  513.7 6.5 %copy-start.60 = (f32[256]{0:T(256)S(1)}, f32[256]{0:T(256)}, u32[]{:S(2)}) copy-start(f32[256]{0:T(256)} %compare_convert_fusion) | copy-start | bytes 3076
  513.7 6.5 %copy-start.70 = (f32[24]{0:T(128)S(1)}, f32[24]{0:T(128)}, u32[]{:S(2)}) copy-start(f32[24]{0:T(128)} %copy-done.68) | copy-start | bytes 292
  513.7 6.5 %copy-start.71 = (f32[256]{0:T(256)S(1)}, f32[256]{0:T(256)}, u32[]{:S(2)}) copy-start(f32[256]{0:T(256)} %get-tuple-element.369) | copy-start | bytes 3076
  513.7 6.6 %copy-start.11 = (bf16[256,1536]{0,1:T(8,128)(2,1)S(1)}, bf16[256,1536]{0,1:T(8,128)(2,1)}, u32[]{:S(2)}) copy-start(bf16[256,1536]{0,1:T(8,128)(2,1)} %copy.259) | copy-start | bytes 2359300
  513.8 8.0 %copy-start.20 = (f32[256,128]{1,0:T(8,128)S(1)}, f32[256,128]{1,0:T(8,128)}, u32[]{:S(2)}) copy-start(f32[256,128]{1,0:T(8,128)} %fusion.77) | copy-start | bytes 393220
  520.2 4.3 copy-start.23
  520.4 5.2 copy-start.42
  532.7 4.6 copy-start.16
  532.7 4.6 copy-start.18
  532.7 4.6 copy-start.27
  532.7 4.6 copy-start.34
  532.7 4.6 copy-start.44
  532.7 4.6 copy-start.54
  532.7 4.6 copy-start.57
  559.1 4.8 copy-start.21
  559.1 7.4 %copy-start.25 = (bf16[512,24]{0,1:T(8,128)(2,1)S(1)}, bf16[512,24]{0,1:T(8,128)(2,1)}, u32[]{:S(2)}) copy-start(bf16[512,24]{0,1:T(8,128)(2,1)} %copy-done.24) | copy-start | bytes 73732
  559.1 8.8 %copy-start.15 = (f32[256,1536]{1,0:T(8,128)S(1)}, f32[256,1536]{1,0:T(8,128)}, u32[]{:S(2)}) copy-start(f32[256,1536]{1,0:T(8,128)} %copy.262) | copy-start | bytes 4718596
  (26 other events, 68.0 us)
Sparse Core Ops, SparseCore 0:
  84.5 203.4 all-gather.7
  290.8 149.5 all-gather.5
  565.6 16.8 all-reduce.12
where the time goes:
time: 603 us; the launch traced here: 593 us
  blocking collectives  165 us (27%)
  waiting for transfers between devices  144 us (24%)
  other arithmetic  108 us (18%)
  local copies, waits for them, and re-layouts  75.7 us (13%)
  matrix products  61.8 us (10%)
  starting transfers between devices  19.6 us (3%)
  between operations  16.9 us (3%)
    all_gather x2, waiting for transfers between devices, entering(): everything = jax.tree.map(lambda part: lax.all_gather(part, axis), value)  126 us
    all_to_all x1, blocking collectives, body(): lax.all_to_all(value_slots, 'seq', split_axis=0, concat_axis=0, tiled=True)  126 us
    select_n x48, other arithmetic, step(): return jax.tree.map(lambda a, b: jnp.where(reached, a, b), new, before)  61.3 us
    all_gather x1, blocking collectives, entering(): everything = jax.tree.map(lambda part: lax.all_gather(part, axis), value)  39.1 us
    dot_general x6, matrix products, block_step(): jnp.einsum('hts,shp->thp', blend_matrix, values_f, precision=tripled)  30.8 us
    scatter x4, local copies, waits for them, and re-layouts, settle(): return jnp.zeros((rows_per_device,) + flat_data.shape[1:], flat_data.dtyp...  16.2 us
    dot_general x6, matrix products, block_step(): jnp.einsum('tn,hpn->thp', read_f, carry_state, precision=tripled)  12.9 us
    another operation x24, other arithmetic  12.2 us
  transfers between devices with their start and end apart: 6, of which 4 were waited for; matrix products, arithmetic and copies ran while one was open for 17% of the time, Pallas kernels for 0%

commit v1 on v0

v1 whole, which is shorter than its diff:
```python
from functools import partial

import jax
import jax.numpy as jnp
from jax import lax
from jax.experimental import pallas as pl
from jax.experimental.pallas import tpu as pltpu
from jax.sharding import PartitionSpec as P

f32 = jnp.float32
bf16 = jnp.bfloat16
LANES = 128
NEG = -1e30
LOG2E = 1.4426950408889634
GROUPS = 1


def split2(x):
    hi = x.astype(bf16)
    return hi, (x - hi.astype(f32)).astype(bf16)


def split3(x):
    hi = x.astype(bf16)
    rest = x - hi.astype(f32)
    mid = rest.astype(bf16)
    return hi, mid, (rest - mid.astype(f32)).astype(bf16)


def mm(a, b):
    return lax.dot_general(a, b, (((1,), (0,)), ((), ())), preferred_element_type=f32)


def mm_nt(a, b):
    return lax.dot_general(a, b, (((1,), (1,)), ((), ())), preferred_element_type=f32)


def iota(shape, dim):
    return lax.broadcasted_iota(jnp.int32, shape, dim)


def params(grid_dims=1):
    return pltpu.CompilerParams(
        dimension_semantics=("arbitrary",) * grid_dims, vmem_limit_bytes=56 * 1024 * 1024
    )


def whole(shape):
    return pl.BlockSpec(shape, lambda *_: (0,) * len(shape))


def dispatch_kernel(shift, capacity, trow_ref, tcol_ref, kaux_ref, oh_ref, ks_ref):
    rows = trow_ref.shape[1]
    slots = oh_ref.shape[0]
    owner_row = lax.shift_right_logical(trow_ref[...], shift)
    owner_col = lax.shift_right_logical(tcol_ref[...], shift)
    earlier = (owner_col == owner_row) & (iota((rows, rows), 0) < iota((rows, rows), 1))
    rank = jnp.sum(jnp.where(earlier, 1.0, 0.0), axis=0, keepdims=True)
    slot = owner_row * capacity + rank.astype(jnp.int32)
    onehot = jnp.where(iota((slots, rows), 0) == slot, 1.0, 0.0).astype(bf16)
    oh_ref[...] = onehot
    ks_ref[...] = mm(onehot, kaux_ref[...]).astype(bf16)


def doc_at(docs_ref, pos):
    start = jnp.int32(0)
    total = pos * 0
    for d in range(docs_ref.shape[0] - 1):
        start = start + docs_ref[d]
        total = total + jnp.where(pos >= start, 1, 0)
    return total


def row_of(ref, c, h):
    return jnp.broadcast_to(ref[c, pl.ds(h, 1), :], (LANES, LANES))


def expand_pair(ref, c, h0):
    upper = iota((LANES, LANES), 0) < LANES // 2
    return jnp.where(upper, row_of(ref, c, h0), row_of(ref, c, h0 + 1)).T


def expand_all(ref, h0):
    return jnp.concatenate([expand_pair(ref, c, h0) for c in range(ref.shape[0])], axis=0)


def setup_kernel(
    heads, lo_count, idx_ref, docs_ref, got_ref, og_ref, bias_ref, dlog_ref,
    pm_ref, b_ref, c_ref, bt_ref, ct_ref, dt_ref, sig_ref, at_ref, btt_ref, eat_ref, wt_ref,
    wdt_ref, mb_ref, keep_ref, u_ref, eadt_ref,
):
    rows = og_ref.shape[0]
    slots = got_ref.shape[0]
    n = b_ref.shape[1]
    chunks = rows // LANES
    j = pl.program_id(0)

    @pl.when(j == 0)
    def _():
        p0 = idx_ref[0] * rows
        aux_t = got_ref[:, 2 * n : 2 * n + LANES].astype(f32).T
        pos = aux_t[LANES - 3 : LANES - 2] * 16.0 + aux_t[LANES - 2 : LANES - 1]
        pos = jnp.where(aux_t[LANES - 1 : LANES] > 0.5, pos, -1.0).astype(jnp.int32)
        pm = jnp.where(iota((rows, slots), 0) == pos, 1.0, 0.0).astype(bf16)
        pm_ref[...] = pm
        placed = mm(pm, got_ref[...])
        b_all = placed[:, :n]
        c_all = placed[:, n : 2 * n]
        b_ref[...] = b_all.astype(bf16)
        c_ref[...] = c_all.astype(bf16)
        logits = placed[:, 2 * n : 2 * n + LANES]
        logits = jnp.where(iota(logits.shape, 1) < heads, logits, 0.0)
        x = logits + bias_ref[...]
        u = jnp.exp(-jnp.abs(x))
        small = u * (1.0 - u * (0.5 - u * (1.0 / 3.0 - u * (0.25 - u * 0.2))))
        dt = jnp.maximum(x, 0.0) + jnp.where(u < 0.03, small, jnp.log(1.0 + u))
        dt_ref[...] = dt
        sig_ref[...] = jnp.where(x >= 0.0, 1.0, u) / (1.0 + u)
        logdt = jnp.log(dt) * LOG2E
        z = dt * (-jnp.exp(dlog_ref[...]) * LOG2E)
        tri = jnp.where(iota((LANES, LANES), 0) >= iota((LANES, LANES), 1), 1.0, 0.0).astype(bf16)
        offs = []
        off = jnp.zeros((1, LANES), f32)
        local = []
        for c in range(chunks):
            z0, z1, z2 = split3(z[c * LANES : (c + 1) * LANES])
            a = (mm(tri, z2) + mm(tri, z1)) + mm(tri, z0)
            local.append(a)
            offs.append(off)
            off = off + a[LANES - 1 : LANES]
        doc_before = doc_at(docs_ref, p0 - 1)
        doc_last = doc_at(docs_ref, p0 + rows - 1)
        for c in range(chunks):
            at = slice(c * LANES, (c + 1) * LANES)
            q0 = p0 + c * LANES
            a = local[c]
            ld = logdt[at]
            end = a[LANES - 1 : LANES]
            doc_n = doc_at(docs_ref, q0 + iota((LANES, LANES), 0))
            doc_t = doc_at(docs_ref, q0 + iota((LANES, LANES), 1))
            causal = (doc_n == doc_t) & (iota((LANES, LANES), 0) >= iota((LANES, LANES), 1))
            mb_ref[at] = jnp.where(causal, 0.0, NEG)
            at_ref[c] = a.T
            btt_ref[c] = (a - ld).T
            eat_ref[c] = jnp.where(doc_n == doc_at(docs_ref, q0 - 1), a, NEG).T
            wt_ref[c] = jnp.where(
                doc_n == doc_at(docs_ref, q0 + LANES - 1), end - a + ld, NEG
            ).T
            full = a + offs[c]
            eadt_ref[c] = jnp.where(doc_n == doc_before, full, NEG).T
            wdt_ref[c] = jnp.where(doc_n == doc_last, off - full + ld, NEG).T
            bt_ref[:, at] = b_all[at].T.astype(bf16)
            ct_ref[:, at] = c_all[at].T.astype(bf16)

    ea = jnp.exp2(expand_all(eadt_ref, 2 * j))
    hi, lo = split2(ea * og_ref[...].astype(f32))
    ut = mm(ct_ref[...], hi) + mm(ct_ref[...], lo)
    keep = jnp.broadcast_to(ea[rows - 1 : rows], (8, LANES))
    keep_ref[...] = keep
    q = n // lo_count
    for k in range(lo_count):
        u_ref[k, :q, :] = ut[k * q : (k + 1) * q]
        u_ref[k, q:, :] = keep


def place_kernel(base, lo_count, got_ref, pm_ref, wdt_ref, bt_ref, keep_ref, v_ref, f_ref):
    rows = pm_ref.shape[0]
    v = mm(pm_ref[...], got_ref[...])
    v_ref[...] = v.astype(bf16)
    w = jnp.exp2(expand_all(wdt_ref, 2 * (base + pl.program_id(0))))
    hi, lo = split2(w * v)
    ft = mm(bt_ref[...], hi) + mm(bt_ref[...], lo)
    q = ft.shape[0] // lo_count
    for k in range(lo_count):
        f_ref[k, :q, :] = ft[k * q : (k + 1) * q]
        f_ref[k, q:, :] = keep_ref[...]


def layer_kernel(
    base, v_ref, g_ref, st_ref, ut_ref, at_ref, btt_ref, eat_ref, wt_ref, b_ref, c_ref,
    bt_ref, ct_ref, mb_ref, skip_ref,
    lout_ref, gval_ref, z_ref, dc_ref, db_ref, gy_ref, vdv_ref, end_ref,
    cb_ref, dvi_ref, ea_ref, w_ref,
):
    rows = v_ref.shape[0]
    chunks = rows // LANES
    half = LANES // 2
    j = pl.program_id(0)
    pair = base + j
    h0 = 2 * pair

    @pl.when(j == 0)
    def _():
        for c in range(chunks):
            at = slice(c * LANES, (c + 1) * LANES)
            cb_ref[at] = mm_nt(c_ref[at], b_ref[at])
        for ref in (z_ref, dc_ref, db_ref, gy_ref, vdv_ref, end_ref):
            ref[...] = jnp.zeros_like(ref)

    lane = iota((LANES, LANES), 1)
    sub = iota((LANES, LANES), 0)
    low = lane < half
    pick = jnp.where(h0 + jnp.where(sub < half, 0, 1) == lane, 1.0, 0.0).astype(bf16)
    skip = skip_ref[0:1]
    st = st_ref[...]
    for c in range(chunks):
        at = slice(c * LANES, (c + 1) * LANES)
        v = v_ref[at]
        g = g_ref[at]
        vf = v.astype(f32)
        gf = g.astype(f32)
        zero = jnp.zeros_like(v)
        gt = gf.T.astype(bf16)
        ea = jnp.exp2(expand_pair(eat_ref, c, h0))
        w = jnp.exp2(expand_pair(wt_ref, c, h0))
        ea_ref[at] = ea
        w_ref[at] = w
        cb = cb_ref[at]
        mb = mb_ref[at]
        zacc = z_ref[at]
        his, los, dvs = [], [], []
        for k in range(2):
            acol = row_of(at_ref, c, h0 + k).T
            spread = jnp.exp2(acol - row_of(btt_ref, c, h0 + k) + mb)
            mine = low if k == 0 else jnp.logical_not(low)
            gv = mm_nt(jnp.where(mine, g, zero), v)
            zacc = zacc + gv * spread
            hi, lo = split2(cb * spread)
            his.append(hi)
            los.append(lo)
            gk = gt[k * half : (k + 1) * half]
            dvs.append(mm(gk, hi) + mm(gk, lo))
        z_ref[at] = zacc
        dvi_ref[at] = jnp.concatenate(dvs, axis=0).T
        both = jnp.concatenate([jnp.where(low, v, zero), jnp.where(low, zero, v)], axis=0)
        y = mm(jnp.concatenate(his, axis=1), both) + mm(jnp.concatenate(los, axis=1), both)
        st_hi, st_lo = split2(st)
        y = y + ea * (mm(c_ref[at], st_hi) + mm(c_ref[at], st_lo))
        lout_ref[at] = (y + skip * vf).astype(bf16)
        p_hi, p_lo = split2(gf * y)
        gy_ref[at] += mm(p_hi, pick) + mm(p_lo, pick)
        eg_hi, eg_lo = split2(ea * gf)
        dc_ref[at] += mm_nt(eg_hi, st_hi) + (mm_nt(eg_hi, st_lo) + mm_nt(eg_lo, st_hi))
        wv_hi, wv_lo = split2(w * vf)
        btc = bt_ref[:, at]
        st = ea[LANES - 1 : LANES] * st + (mm(btc, wv_hi) + mm(btc, wv_lo))
    ut = ut_ref[...]
    final = jnp.sum(st * ut, axis=0, keepdims=True)
    e0, e1, e2 = split3(jnp.broadcast_to(final, (8, LANES)))
    end_ref[...] += (mm(e2, pick) + mm(e1, pick)) + mm(e0, pick)
    for c in reversed(range(chunks)):
        at = slice(c * LANES, (c + 1) * LANES)
        vf = v_ref[at].astype(f32)
        gf = g_ref[at].astype(f32)
        ea = ea_ref[at]
        w = w_ref[at]
        ut_hi, ut_lo = split2(ut)
        dv = dvi_ref[at] + w * (mm(b_ref[at], ut_hi) + mm(b_ref[at], ut_lo))
        gval_ref[at] = (dv + skip * gf).astype(bf16)
        p_hi, p_lo = split2(vf * dv)
        vdv_ref[at] += mm(p_hi, pick) + mm(p_lo, pick)
        wv_hi, wv_lo = split2(w * vf)
        db_ref[at] += mm_nt(wv_hi, ut_hi) + (mm_nt(wv_hi, ut_lo) + mm_nt(wv_lo, ut_hi))
        eg_hi, eg_lo = split2(ea * gf)
        ctc = ct_ref[:, at]
        ut = ea[LANES - 1 : LANES] * ut + (mm(ctc, eg_hi) + mm(ctc, eg_lo))


def finish_kernel(count, *refs):
    parts = [refs[6 * i : 6 * i + 6] for i in range(count)]
    b_ref, c_ref, dt_ref, sig_ref, dlog_ref, glog_ref, keys_ref = refs[6 * count :]
    rows = b_ref.shape[0]
    n = b_ref.shape[1]
    heads = glog_ref.shape[1]

    def total(i, at):
        out = parts[0][i][at]
        for part in parts[1:]:
            out = out + part[i][at]
        return out

    rate = -jnp.exp(dlog_ref[...])
    tri = jnp.where(iota((LANES, LANES), 0) <= iota((LANES, LANES), 1), 1.0, 0.0).astype(bf16)
    off = total(5, slice(0, 1))
    for c in reversed(range(rows // LANES)):
        at = slice(c * LANES, (c + 1) * LANES)
        vdv = total(4, at)
        q0, q1, q2 = split3(total(3, at) - vdv)
        run = (mm(tri, q2) + mm(tri, q1)) + mm(tri, q0) + off
        off = run[0:1]
        glog = (vdv / dt_ref[at] + rate * run) * sig_ref[at]
        glog_ref[at] = glog[:, :heads]
        z = total(0, at)
        z_hi, z_lo = split2(z)
        t_hi, t_lo = split2(z.T)
        keys_ref[at, n:] = total(1, at) + (mm(z_hi, b_ref[at]) + mm(z_lo, b_ref[at]))
        keys_ref[at, :n] = total(2, at) + (mm(t_hi, c_ref[at]) + mm(t_lo, c_ref[at]))


def exchange(payload, init, lo_count, hi_count, reverse):
    size = lo_count * hi_count
    q = payload.shape[1] - 8
    groups = [[z * lo_count + k for k in range(lo_count)] for z in range(hi_count)]
    parts = lax.all_to_all(
        payload, "seq", split_axis=0, concat_axis=0, tiled=True, axis_index_groups=groups
    )
    order = list(range(lo_count))
    if reverse:
        order = order[::-1]
    state = parts[order[0], :q]
    keep = parts[order[0], q : q + 8]
    for k in order[1:]:
        state = parts[k, q : q + 1] * state + parts[k, :q]
        keep = parts[k, q : q + 8] * keep
    mine = jnp.concatenate([state, keep], axis=0)
    z = lax.axis_index("seq") // lo_count
    got = []
    for e in range(1, hi_count):
        step = -e * lo_count if reverse else e * lo_count
        perm = [(i, i + step) for i in range(size) if 0 <= i + step < size]
        got.append(lax.ppermute(mine, "seq", perm))
    acc = init
    for e in range(hi_count - 1, 0, -1):
        there = (z + e < hi_count) if reverse else (z - e >= 0)
        other = got[e - 1]
        acc = jnp.where(there, other[q : q + 1] * acc + other[:q], acc)
    starts = [None] * lo_count
    for k in order:
        starts[k] = acc
        acc = parts[k, q : q + 1] * acc + parts[k, :q]
    out = lax.all_to_all(
        jnp.stack(starts), "seq", split_axis=0, concat_axis=0, tiled=True, axis_index_groups=groups
    )
    return out.reshape(lo_count * q, out.shape[2])


def body(
    token_values, step_logits, write_keys, read_queries, target, doc_lengths,
    decay_log, step_bias, skip_gain, init_state, out_grad,
):
    rows = token_values.shape[0]
    size = lax.axis_size("seq")
    me = lax.axis_index("seq")
    heads = decay_log.shape[0]
    width = token_values.shape[1]
    head_width = width // heads
    n = write_keys.shape[1]
    capacity = 2 * rows // size
    slots = size * capacity
    pairs = width // LANES
    assert head_width * 2 == LANES and n == LANES and heads <= LANES - 3
    assert rows & (rows - 1) == 0 and rows % LANES == 0
    lo_count = 4 if size % 4 == 0 else 1
    hi_count = size // lo_count
    q = n // lo_count

    local = target % rows
    marks = jnp.stack([local // 16, local % 16, jnp.ones_like(local)], axis=1).astype(bf16)
    kaux = jnp.concatenate(
        [
            write_keys,
            read_queries,
            step_logits,
            jnp.zeros((rows, LANES - 3 - heads), bf16),
            marks,
        ],
        axis=1,
    )
    kw = kaux.shape[1]
    onehot, kslots = pl.pallas_call(
        partial(dispatch_kernel, rows.bit_length() - 1, capacity),
        out_shape=(
            jax.ShapeDtypeStruct((slots, rows), bf16),
            jax.ShapeDtypeStruct((slots, kw), bf16),
        ),
        compiler_params=pltpu.CompilerParams(vmem_limit_bytes=56 * 1024 * 1024),
        name="dispatch",
    )(target.reshape(1, rows), target.reshape(rows, 1), kaux)

    def route(x):
        wide = x.reshape(size, capacity, x.shape[1])
        wide = lax.all_to_all(wide, "seq", split_axis=0, concat_axis=0, tiled=True)
        return wide.reshape(slots, x.shape[1])

    got_keys = route(kslots)
    count = min(GROUPS, pairs)
    edges = [pairs * i // count for i in range(count + 1)]
    spans = list(zip(edges[:-1], edges[1:]))
    got_values = []
    for lower, upper in spans:
        part = token_values[:, lower * LANES : upper * LANES]
        got_values.append(route(jnp.dot(onehot, part, preferred_element_type=f32).astype(bf16)))

    pad = (0, LANES - heads)
    bias_row = jnp.pad(step_bias, pad).reshape(1, LANES)
    dlog_row = jnp.pad(decay_log, pad).reshape(1, LANES)
    skip_row = jnp.broadcast_to(jnp.repeat(skip_gain, head_width)[None, :], (8, width))
    idx = jnp.reshape(me, (1,)).astype(jnp.int32)
    smem = pl.BlockSpec(memory_space=pltpu.SMEM)
    col = pl.BlockSpec((rows, LANES), lambda j: (0, j))
    tiles = whole((rows // LANES, LANES, LANES))

    def sds(shape, dtype=f32):
        return jax.ShapeDtypeStruct(shape, dtype)

    (pm, b, c, bt, ct, dt, sig, at, btt, eat, wt, wdt, mb, keep, u_span) = pl.pallas_call(
        partial(setup_kernel, heads, lo_count),
        grid=(pairs,),
        in_specs=[smem, smem, whole((slots, kw)), col, whole((1, LANES)), whole((1, LANES))],
        out_specs=[
            whole((rows, slots)),
            whole((rows, n)), whole((rows, n)), whole((n, rows)), whole((n, rows)),
            whole((rows, LANES)), whole((rows, LANES)),
            tiles, tiles, tiles, tiles, tiles,
            whole((rows, LANES)),
            pl.BlockSpec((8, LANES), lambda j: (0, j)),
            pl.BlockSpec((lo_count, q + 8, LANES), lambda j: (0, 0, j)),
        ],
        out_shape=[
            sds((rows, slots), bf16),
            sds((rows, n), bf16), sds((rows, n), bf16), sds((n, rows), bf16), sds((n, rows), bf16),
            sds((rows, LANES)), sds((rows, LANES)),
            *[sds((rows // LANES, LANES, LANES))] * 5,
            sds((rows, LANES)),
            sds((8, width)),
            sds((lo_count, q + 8, width)),
        ],
        scratch_shapes=[pltpu.VMEM((rows // LANES, LANES, LANES), f32)],
        compiler_params=params(),
        name="setup",
    )(idx, doc_lengths, got_keys, out_grad, bias_row, dlog_row)

    lo_at = me % lo_count
    init_part = lax.dynamic_slice_in_dim(init_state, lo_at * q, q, axis=2)
    init_part = init_part.reshape(width, q).T
    zero_part = jnp.zeros_like(init_part)
    ut = exchange(u_span, zero_part, lo_count, hi_count, True)

    partials = []
    outs = []
    grads = []
    for (lower, upper), got in zip(spans, got_values):
        cols = (upper - lower) * LANES
        shifted = pl.BlockSpec((rows, LANES), lambda j, lower=lower: (0, lower + j))
        v, f_span = pl.pallas_call(
            partial(place_kernel, lower, lo_count),
            grid=(upper - lower,),
            in_specs=[
                pl.BlockSpec((slots, LANES), lambda j: (0, j)),
                whole((rows, slots)),
                tiles,
                whole((n, rows)),
                pl.BlockSpec((8, LANES), lambda j, lower=lower: (0, lower + j)),
            ],
            out_specs=[col, pl.BlockSpec((lo_count, q + 8, LANES), lambda j: (0, 0, j))],
            out_shape=[sds((rows, cols), bf16), sds((lo_count, q + 8, cols))],
            compiler_params=params(),
            name="place",
        )(got, pm, wdt, bt, keep)
        st = exchange(
            f_span, init_part[:, lower * LANES : upper * LANES], lo_count, hi_count, False
        )
        acc = whole((rows, LANES))
        res = pl.pallas_call(
            partial(layer_kernel, lower),
            grid=(upper - lower,),
            in_specs=[
                col,
                shifted,
                pl.BlockSpec((n, LANES), lambda j: (0, j)),
                pl.BlockSpec((n, LANES), lambda j, lower=lower: (0, lower + j)),
                tiles, tiles, tiles, tiles,
                whole((rows, n)), whole((rows, n)), whole((n, rows)), whole((n, rows)),
                whole((rows, LANES)),
                pl.BlockSpec((8, LANES), lambda j, lower=lower: (0, lower + j)),
            ],
            out_specs=[col, col, acc, acc, acc, acc, acc, whole((8, LANES))],
            out_shape=[
                sds((rows, cols), bf16), sds((rows, cols), bf16),
                sds((rows, LANES)), sds((rows, LANES)), sds((rows, LANES)),
                sds((rows, LANES)), sds((rows, LANES)), sds((8, LANES)),
            ],
            scratch_shapes=[pltpu.VMEM((rows, LANES), f32)] * 4,
            compiler_params=params(),
            name="layer",
        )(v, out_grad, st, ut, at, btt, eat, wt, b, c, bt, ct, mb, skip_row)
        outs.append(res[0])
        grads.append(res[1])
        partials.extend(res[2:])

    grad_logits, keys_grad = pl.pallas_call(
        partial(finish_kernel, count),
        out_shape=[sds((rows, heads)), sds((rows, 2 * n))],
        compiler_params=pltpu.CompilerParams(vmem_limit_bytes=56 * 1024 * 1024),
        name="finish",
    )(*partials, b, c, dt, sig, dlog_row)
    if lax.axis_size("head") == 2:
        keys_grad = keys_grad + lax.ppermute(keys_grad, "head", [(0, 1), (1, 0)])
    else:
        keys_grad = lax.psum(keys_grad, "head")
    layer_out = outs[0] if count == 1 else jnp.concatenate(outs, axis=1)
    grad_values = grads[0] if count == 1 else jnp.concatenate(grads, axis=1)
    return layer_out, grad_values, grad_logits, keys_grad[:, :n], keys_grad[:, n:]


def solution(mesh):
    return jax.shard_map(
        body,
        mesh=mesh,
        in_specs=(
            P("seq", "head"),
            P("seq", "head"),
            P("seq", None),
            P("seq", None),
            P("seq"),
            P(),
            P("head"),
            P("head"),
            P("head"),
            P("head", None, None),
            P("seq", "head"),
        ),
        out_specs=(
            P("seq", "head"),
            P("seq", "head"),
            P("seq", "head"),
            P("seq", None),
            P("seq", None),
        ),
        check_vma=False,
    )
```

time: 603 us -> 283 us (0.47)
  blocking collectives: 165 us -> 0 us
  other arithmetic: 108 us -> 11.5 us
  Pallas kernels: 0 us -> 69.3 us
  local copies, waits for them, and re-layouts: 75.7 us -> 18.1 us
  matrix products: 61.8 us -> 4.69 us
  starting transfers between devices: 19.6 us -> 43.2 us
  between operations: 16.9 us -> 0.96 us
  waiting for transfers between devices: 144 us -> 131 us
    all_gather x2 -> x0, waiting for transfers between devices: 126 us -> none  [entering(): everything = jax.tree.map(lambda part: lax.all_gather(part, axis), value)]
    all_to_all x1 -> x0, blocking collectives: 126 us -> none  [body(): lax.all_to_all(value_slots, 'seq', split_axis=0, concat_axis=0, tiled=True)]
    ppermute x0 -> x7, waiting for transfers between devices: none -> 86.6 us  [the longest x6 86.1 us: exchange(): got.append(lax.ppermute(mine, 'seq', perm))]
    pallas_call x0 -> x5, Pallas kernels: none -> 69.3 us  [the longest x1 39 us: body(): pl.pallas_call(partial(layer_kernel, lower), grid=(upper - lower,), in_sp...]
    select_n x51 -> x0, other arithmetic: 62.7 us -> none  [the longest x48 61.3 us: step(): return jax.tree.map(lambda a, b: jnp.where(reached, a, b), new, before)]
    dot_general x24 -> x1, matrix products: 61.8 us -> 4.69 us  [body(): jnp.dot(onehot, part, preferred_element_type=f32).astype(bf16)]
    all_gather x1 -> x0, blocking collectives: 39.1 us -> none  [entering(): everything = jax.tree.map(lambda part: lax.all_gather(part, axis), value)]
    all_to_all x3 -> x6, waiting for transfers between devices: 6.32 us -> 43.9 us  [the longest x2 19.1 us: route(): wide = lax.all_to_all(wide, 'seq', split_axis=0, concat_axis=0, tiled=True)]
  transfers between devices with their start and end apart: 6 -> 13, of which waited for: 4 -> 7; matrix products, arithmetic and copies ran while one was open for 17% -> 8% of each run, Pallas kernels for 0% -> 0%
where the time goes in v1:
time: 283 us; the launch traced here: 278 us
  waiting for transfers between devices  131 us (46%)
  Pallas kernels  69.3 us (24%)
  starting transfers between devices  43.2 us (15%)
  local copies, waits for them, and re-layouts  18.1 us (6%)
  other arithmetic  11.5 us (4%)
  matrix products  4.69 us (2%)
    ppermute x6, waiting for transfers between devices, exchange(): got.append(lax.ppermute(mine, 'seq', perm))  86.1 us
    pallas_call x1, Pallas kernels, body(): pl.pallas_call(partial(layer_kernel, lower), grid=(upper - lower,), in_sp...  39 us
    all_to_all x2, waiting for transfers between devices, route(): wide = lax.all_to_all(wide, 'seq', split_axis=0, concat_axis=0, tiled=True)  19.1 us
    all_to_all x2, waiting for transfers between devices, exchange(): lax.all_to_all(payload, 'seq', split_axis=0, concat_axis=0, tiled=True, a...  14.9 us
    ppermute x6, starting transfers between devices, exchange(): got.append(lax.ppermute(mine, 'seq', perm))  14.8 us
    all_to_all x2, starting transfers between devices, route(): wide = lax.all_to_all(wide, 'seq', split_axis=0, concat_axis=0, tiled=True)  14 us
    pallas_call x1, Pallas kernels, body(): pl.pallas_call(partial(place_kernel, lower, lo_count), grid=(upper - lowe...  12.3 us
    pallas_call x1, Pallas kernels, body(): pl.pallas_call(partial(setup_kernel, heads, lo_count), grid=(pairs,), in_...  12.1 us
  transfers between devices with their start and end apart: 13, of which 7 were waited for; matrix products, arithmetic and copies ran while one was open for 8% of the time, Pallas kernels for 0%

profile of v1, /device:TPU:0, one launch (start us, length us, event | category | flops | bytes accessed | tf_op | source)
XLA Modules:
  0.0 278.2 jit_solution(17996784826063197183)
XLA Ops:
  0.6 0.0 copy-start
  0.6 0.8 fusion.19
  1.5 1.5 copy.22.tcol_ref
  3.0 0.9 copy.19
  3.9 0.1 stack.52
  4.0 0.1 stack.53
  4.2 0.0 copy-start.13
  4.2 1.9 concatenate.10.kaux_ref
  6.1 3.0 %dispatch.1 = (bf16[1024,512]{1,0:T(8,128)(2,1)}, bf16[1024,384]{1,0:T(8,128)(2,1)}) custom-call(s32[1,512]{1,0:T(1,128)} %bitcast.107, s32[512,1]{1,0:T(8,128)} %copy.22.tcol_ref, bf16[512,384]{1,0:T(8,128)(2,1)} %concatenate.10.kaux_ref), custom_call_target="tpu_custom_call" | custom-call | tf_op jit(solution)/shard_map/dispatch/pallas_call | solution.py:370
  9.1 8.3 %all-to-all-start.1 = ((bf16[16,64,384]{2,1,0:T(8,128)(2,1)}), bf16[16,64,384]{2,1,0:T(8,128)(2,1)S(1)}, u32[]{:S(2)}, u32[]{:S(2)}) async-start(bf16[16,64,384]{2,1,0:T(8,128)(2,1)} %bitcast.104), calls=%async_computation.1 | async-start | bytes 1572864 | tf_op jit(solution)/shard_map/all_to_all | solution.py:382
  17.5 0.6 pad_bitcast_fusion
  18.1 19.1 %all-to-all-done.1 = bf16[16,64,384]{2,1,0:T(8,128)(2,1)S(1)} async-done(((bf16[16,64,384]{2,1,0:T(8,128)(2,1)}), bf16[16,64,384]{2,1,0:T(8,128)(2,1)S(1)}, u32[]{:S(2)}, u32[]{:S(2)}) %all-to-all-start.1) | async-done | bytes 786464 | tf_op jit(solution)/shard_map/all_to_all | solution.py:382
  37.2 0.9 copy-done.3
  38.1 12.1 %setup.1 = (bf16[512,1024]{1,0:T(8,128)(2,1)}, bf16[512,128]{1,0:T(8,128)(2,1)}, bf16[512,128]{1,0:T(8,128)(2,1)}, bf16[128,512]{1,0:T(8,128)(2,1)}, bf16[128,51...) custom-call(s32[1]{0:T(128)} %bitcast.4.idx_ref, ...), custom_call_target="tpu_custom_call" | custom-call | tf_op jit(solution)/shard_map/setup/pallas_call | solution.py:406
  50.2 3.5 %all-to-all-start.4 = ((f32[4,40,1536]{2,1,0:T(8,128)}), f32[4,40,1536]{2,1,0:T(8,128)S(1)}, u32[]{:S(2)}, u32[]{:S(2)}) async-start(f32[4,40,1536]{2,1,0:T(8,128)} %get-tuple-element.42), calls=%async_computation.4 | async-start | bytes 1966080 | tf_op jit(solution)/shard_map/all_to_all | solution.py:304
  53.7 4.7 %convolution_convert_fusion = bf16[1024,1536]{1,0:T(8,128)(2,1)} fusion(bf16[1024,512]{1,0:T(8,128)(2,1)} %get-tuple-element.34, bf16[512,1536]{1,0:T(8,128)(2,1)S(1)} %copy-done), kind=kOutput, calls=%fused_computation | convolution fusion | flops 1612185600 | bytes 5767168 | tf_op jit(solution)/shard_map/dot_general | solution.py:392
  58.4 6.3 %all-to-all-done.4 = f32[4,40,1536]{2,1,0:T(8,128)S(1)} async-done(((f32[4,40,1536]{2,1,0:T(8,128)}), f32[4,40,1536]{2,1,0:T(8,128)S(1)}, u32[]{:S(2)}, u32[]{:S(2)}) %all-to-all-start.4) | async-done | bytes 983072 | tf_op jit(solution)/shard_map/all_to_all | solution.py:304
  64.7 5.7 %all-to-all-start = ((bf16[16,64,1536]{2,1,0:T(8,128)(2,1)}), bf16[16,64,1536]{2,1,0:T(8,128)(2,1)}, u32[]{:S(2)}, u32[]{:S(2)}) async-start(bf16[16,64,1536]{2,1,0:T(8,128)(2,1)} %bitcast.98), calls=%async_computation | async-start | bytes 6291456 | tf_op jit(solution)/shard_map/all_to_all | solution.py:382
  70.4 0.1 slice_reduce_fusion.3
  70.5 0.1 fusion.3
  70.5 0.7 pad_maximum_fusion.3
  71.2 1.3 collective-permute-start.4
  72.5 1.3 collective-permute-start.3
  73.9 1.3 collective-permute-start.5
  75.2 1.4 constant_dynamic-slice_fusion
  76.6 0.9 copy.25
  77.5 79.2 %collective-permute-done.4 = f32[40,1536]{1,0:T(8,128)} collective-permute-done((f32[40,1536]{1,0:T(8,128)}, f32[40,1536]{1,0:T(8,128)}, u32[]{:S(2)}, u32[]{:S(2)}) %collective-permute-start.4) | collective-permute-done | bytes 245792 | tf_op jit(solution)/shard_map/ppermute | solution.py:321
  156.7 1.4 slice_reduce_fusion
  158.1 1.4 slice_reduce_fusion.1
  159.5 1.4 fusion.16
  160.9 12.3 %place.1 = (bf16[512,1536]{1,0:T(8,128)(2,1)}, f32[4,40,1536]{2,1,0:T(8,128)}) custom-call(bf16[1024,1536]{1,0:T(8,128)(2,1)} %bitcast.3.got_ref, bf16[512,1024]{1,0:T(8,128)(2,1)} %get-tuple-element.36.pm_ref, f32[4,128,128]{2,1,0:T(8,128)} %get-tuple-element.37.wdt_ref, bf16[128,512]{1,0:T(8,128)(2,1)} %get-tuple-element.38.bt_ref, ...), custom_call_target="tpu_custom_call" | custom-call | tf_op jit(solution)/shard_map/place/pallas_call | solution.py:445
  173.3 3.8 %all-to-all-start.2 = ((f32[4,40,1536]{2,1,0:T(8,128)}), f32[4,40,1536]{2,1,0:T(8,128)S(1)}, u32[]{:S(2)}, u32[]{:S(2)}) async-start(f32[4,40,1536]{2,1,0:T(8,128)} %get-tuple-element.41), calls=%async_computation.2 | async-start | bytes 1966080 | tf_op jit(solution)/shard_map/all_to_all | solution.py:304
  177.1 2.0 add_bitcast_fusion
  179.1 0.7 copy-done.4
  179.7 0.7 fusion.9
  180.5 8.5 %all-to-all-done.2 = f32[4,40,1536]{2,1,0:T(8,128)S(1)} async-done(((f32[4,40,1536]{2,1,0:T(8,128)}), f32[4,40,1536]{2,1,0:T(8,128)S(1)}, u32[]{:S(2)}, u32[]{:S(2)}) %all-to-all-start.2) | async-done | bytes 983072 | tf_op jit(solution)/shard_map/all_to_all | solution.py:304
  189.0 0.1 slice_reduce_fusion.6
  189.1 0.1 fusion.7
  189.2 0.7 pad_maximum_fusion.2
  189.9 7.0 %collective-permute-start = (f32[40,1536]{1,0:T(8,128)}, f32[40,1536]{1,0:T(8,128)}, u32[]{:S(2)}, u32[]{:S(2)}) collective-permute-start(f32[40,1536]{1,0:T(8,128)} %pad_maximum_fusion.2), channel_id=1, source_target_pairs={{0,8},{2,10},{4,12},{6,14},{8,16},{10,18},{12,20},{14,22},{16,24},... | collective-permute-start | bytes 737288 | tf_op jit(solution)/shard_map/ppermute | solution.py:321
  196.9 2.0 collective-permute-start.1
  198.9 2.0 collective-permute-start.2
  200.9 0.9 pad_maximum_fusion.1
  201.8 3.5 %all-to-all-start.5 = ((f32[4,32,1536]{2,1,0:T(8,128)}), f32[4,32,1536]{2,1,0:T(8,128)S(1)}, u32[]{:S(2)}, u32[]{:S(2)}) async-start(f32[4,32,1536]{2,1,0:T(8,128)} %pad_maximum_fusion.1), calls=%async_computation.5 | async-start | bytes 1572864 | tf_op jit(solution)/shard_map/all_to_all | solution.py:331
  205.3 6.9 %collective-permute-done.2 = f32[40,1536]{1,0:T(8,128)} collective-permute-done((f32[40,1536]{1,0:T(8,128)}, f32[40,1536]{1,0:T(8,128)}, u32[]{:S(2)}, u32[]{:S(2)}) %collective-permute-start.2) | collective-permute-done | bytes 245792 | tf_op jit(solution)/shard_map/ppermute | solution.py:321
  212.2 0.8 slice_reduce_fusion.7
  213.1 0.8 slice_reduce_fusion.8
  213.9 0.8 slice_reduce_fusion.9
  214.7 1.3 fusion.8
  216.0 0.8 add_bitcast_fusion.1
  216.8 0.0 copy-start.11
  216.8 0.9 pad_maximum_fusion
  217.8 3.5 %all-to-all-start.3 = ((f32[4,32,1536]{2,1,0:T(8,128)}), f32[4,32,1536]{2,1,0:T(8,128)S(1)}, u32[]{:S(2)}, u32[]{:S(2)}) async-start(f32[4,32,1536]{2,1,0:T(8,128)} %pad_maximum_fusion), calls=%async_computation.3 | async-start | bytes 1572864 | tf_op jit(solution)/shard_map/all_to_all | solution.py:331
  221.3 0.1 broadcast_in_dim.21
  221.3 0.1 broadcast_in_dim.22
  221.4 10.0 %all-to-all-done.3 = f32[4,32,1536]{2,1,0:T(8,128)S(1)} async-done(((f32[4,32,1536]{2,1,0:T(8,128)}), f32[4,32,1536]{2,1,0:T(8,128)S(1)}, u32[]{:S(2)}, u32[]{:S(2)}) %all-to-all-start.3) | async-done | bytes 786464 | tf_op jit(solution)/shard_map/all_to_all | solution.py:331
  231.4 0.7 broadcast_in_dim.23.skip_ref
  232.1 0.2 copy-done.2
  232.3 39.0 %layer.1 = (bf16[512,1536]{1,0:T(8,128)(2,1)}, bf16[512,1536]{1,0:T(8,128)(2,1)}, f32[512,128]{1,0:T(8,128)}, f32[512,128]{1,0:T(8,128)}, f32[512,128]{1,0:T(8,1...) custom-call(bf16[512,1536]{1,0:T(8,128)(2,1)} %get-tuple-element.40.v_ref, ...), custom_call_target="tpu_custom_call" | custom-call | tf_op jit(solution)/shard_map/layer/pallas_call | solution.py:464
  271.4 2.8 %finish.1 = (f32[512,24]{1,0:T(8,128)}, f32[512,256]{1,0:T(8,128)}) custom-call(f32[512,128]{1,0:T(8,128)} %get-tuple-element.53.refs_0_, f32[512,128]{1,0:T(8,128)} %get-tuple-element.54.refs_1_, f32[512,128]{1,0:T(8,128)} %get-tuple-element.55.refs_2_, f32[512,128]{1,0:T(8,128)} %get-tuple-element.56.refs_3_, f32[512,128]{1,0:T(8,128)} %get-tuple-element.57.refs_4_, ...), custom_call_target="tpu_custom_call" | custom-call | tf_op jit(solution)/shard_map/finish/pallas_call | solution.py:491
  274.2 1.7 copy.24
  275.9 0.4 collective-permute-done.6
  276.3 1.1 add.117
  277.4 0.8 fusion.23
  (33 shorter events, 0.1 us)
Async XLA Ops:
  0.6 53.0 %copy-start = (bf16[512,1536]{1,0:T(8,128)(2,1)S(1)}, bf16[512,1536]{1,0:T(8,128)(2,1)}, u32[]{:S(2)}) copy-start(bf16[512,1536]{1,0:T(8,128)(2,1)} %param.11) | copy-start | bytes 4718596
  4.2 13.3 %copy-start.12 = (f32[24]{0:T(128)S(1)}, f32[24]{0:T(128)}, u32[]{:S(2)}) copy-start(f32[24]{0:T(128)} %param.17) | copy-start | bytes 292
  4.2 13.3 %copy-start.13 = (f32[24]{0:T(128)S(1)}, f32[24]{0:T(128)}, u32[]{:S(2)}) copy-start(f32[24]{0:T(128)} %param.18) | copy-start | bytes 292
  9.1 28.0 %all-to-all-start.1 = ((bf16[16,64,384]{2,1,0:T(8,128)(2,1)}), bf16[16,64,384]{2,1,0:T(8,128)(2,1)S(1)}, u32[]{:S(2)}, u32[]{:S(2)}) async-start(bf16[16,64,384]{2,1,0:T(8,128)(2,1)} %bitcast.104), calls=%async_computation.1 | async-start | bytes 1572864 | tf_op jit(solution)/shard_map/all_to_all | solution.py:382
  37.2 0.9 copy-start.3
  50.2 14.5 %all-to-all-start.4 = ((f32[4,40,1536]{2,1,0:T(8,128)}), f32[4,40,1536]{2,1,0:T(8,128)S(1)}, u32[]{:S(2)}, u32[]{:S(2)}) async-start(f32[4,40,1536]{2,1,0:T(8,128)} %get-tuple-element.42), calls=%async_computation.4 | async-start | bytes 1966080 | tf_op jit(solution)/shard_map/all_to_all | solution.py:304
  64.7 96.3 %all-to-all-start = ((bf16[16,64,1536]{2,1,0:T(8,128)(2,1)}), bf16[16,64,1536]{2,1,0:T(8,128)(2,1)}, u32[]{:S(2)}, u32[]{:S(2)}) async-start(bf16[16,64,1536]{2,1,0:T(8,128)(2,1)} %bitcast.98), calls=%async_computation | async-start | bytes 6291456 | tf_op jit(solution)/shard_map/all_to_all | solution.py:382
  70.4 3.4 %copy-start.9 = (f32[1536]{0:T(1024)}, f32[1536]{0:T(1024)S(1)}, u32[]{:S(2)}) copy-start(f32[1536]{0:T(1024)S(1)} %get-tuple-element.76) | copy-start | bytes 18436
  71.2 85.5 %collective-permute-start.4 = (f32[40,1536]{1,0:T(8,128)}, f32[40,1536]{1,0:T(8,128)}, u32[]{:S(2)}, u32[]{:S(2)}) collective-permute-start(f32[40,1536]{1,0:T(8,128)} %pad_maximum_fusion.3), channel_id=1, source_target_pairs={{16,0},{18,2},{20,4},{22,6},{24,8},{26,10},{28,12},{30,14},{17,1},... | collective-permute-start | bytes 737288 | tf_op jit(solution)/shard_map/ppermute | solution.py:321
  72.5 85.6 %collective-permute-start.3 = (f32[40,1536]{1,0:T(8,128)}, f32[40,1536]{1,0:T(8,128)}, u32[]{:S(2)}, u32[]{:S(2)}) collective-permute-start(f32[40,1536]{1,0:T(8,128)} %pad_maximum_fusion.3), channel_id=1, source_target_pairs={{8,0},{10,2},{12,4},{14,6},{16,8},{18,10},{20,12},{22,14},{24,16},... | collective-permute-start | bytes 737288 | tf_op jit(solution)/shard_map/ppermute | solution.py:321
  73.9 85.7 %collective-permute-start.5 = (f32[40,1536]{1,0:T(8,128)}, f32[40,1536]{1,0:T(8,128)}, u32[]{:S(2)}, u32[]{:S(2)}) collective-permute-start(f32[40,1536]{1,0:T(8,128)} %pad_maximum_fusion.3), channel_id=1, source_target_pairs={{24,0},{26,2},{28,4},{30,6},{25,1},{27,3},{29,5},{31,7}} | collective-permute-start | bytes 737288 | tf_op jit(solution)/shard_map/ppermute | solution.py:321
  173.3 15.7 %all-to-all-start.2 = ((f32[4,40,1536]{2,1,0:T(8,128)}), f32[4,40,1536]{2,1,0:T(8,128)S(1)}, u32[]{:S(2)}, u32[]{:S(2)}) async-start(f32[4,40,1536]{2,1,0:T(8,128)} %get-tuple-element.41), calls=%async_computation.2 | async-start | bytes 1966080 | tf_op jit(solution)/shard_map/all_to_all | solution.py:304
  179.1 0.7 copy-start.4
  180.4 20.4 %copy-start.5 = (f32[32,1536]{1,0:T(8,128)S(1)}, f32[32,1536]{1,0:T(8,128)}, u32[]{:S(2)}) copy-start(f32[32,1536]{1,0:T(8,128)} %copy-done.4) | copy-start | bytes 589828
  180.4 20.4 %copy-start.6 = (f32[1,32,1536]{2,1,0:T(8,128)S(1)}, f32[1,32,1536]{2,1,0:T(8,128)}, u32[]{:S(2)}) copy-start(f32[1,32,1536]{2,1,0:T(8,128)} %fusion.9) | copy-start | bytes 589828
  180.5 20.4 %copy-start.7 = (f32[1,32,1536]{2,1,0:T(8,128)S(1)}, f32[1,32,1536]{2,1,0:T(8,128)}, u32[]{:S(2)}) copy-start(f32[1,32,1536]{2,1,0:T(8,128)} %get-tuple-element.81) | copy-start | bytes 589828
  180.5 20.4 %copy-start.8 = (f32[32,1536]{1,0:T(8,128)S(1)}, f32[32,1536]{1,0:T(8,128)}, u32[]{:S(2)}) copy-start(f32[32,1536]{1,0:T(8,128)} %get-tuple-element.82) | copy-start | bytes 589828
  189.1 0.8 copy-start.10
  189.9 24.0 %collective-permute-start = (f32[40,1536]{1,0:T(8,128)}, f32[40,1536]{1,0:T(8,128)}, u32[]{:S(2)}, u32[]{:S(2)}) collective-permute-start(f32[40,1536]{1,0:T(8,128)} %pad_maximum_fusion.2), channel_id=1, source_target_pairs={{0,8},{2,10},{4,12},{6,14},{8,16},{10,18},{12,20},{14,22},{16,24},... | collective-permute-start | bytes 737288 | tf_op jit(solution)/shard_map/ppermute | solution.py:321
  196.9 16.2 %collective-permute-start.1 = (f32[40,1536]{1,0:T(8,128)}, f32[40,1536]{1,0:T(8,128)}, u32[]{:S(2)}, u32[]{:S(2)}) collective-permute-start(f32[40,1536]{1,0:T(8,128)} %pad_maximum_fusion.2), channel_id=1, source_target_pairs={{0,16},{2,18},{4,20},{6,22},{8,24},{10,26},{12,28},{14,30},{1,17},... | collective-permute-start | bytes 737288 | tf_op jit(solution)/shard_map/ppermute | solution.py:321
  198.9 13.4 %collective-permute-start.2 = (f32[40,1536]{1,0:T(8,128)}, f32[40,1536]{1,0:T(8,128)}, u32[]{:S(2)}, u32[]{:S(2)}) collective-permute-start(f32[40,1536]{1,0:T(8,128)} %pad_maximum_fusion.2), channel_id=1, source_target_pairs={{0,24},{2,26},{4,28},{6,30},{1,25},{3,27},{5,29},{7,31}} | collective-permute-start | bytes 737288 | tf_op jit(solution)/shard_map/ppermute | solution.py:321
  201.8 15.9 %all-to-all-start.5 = ((f32[4,32,1536]{2,1,0:T(8,128)}), f32[4,32,1536]{2,1,0:T(8,128)S(1)}, u32[]{:S(2)}, u32[]{:S(2)}) async-start(f32[4,32,1536]{2,1,0:T(8,128)} %pad_maximum_fusion.1), calls=%async_computation.5 | async-start | bytes 1572864 | tf_op jit(solution)/shard_map/all_to_all | solution.py:331
  216.8 4.5 %copy-start.11 = (f32[24]{0:T(128)S(1)}, f32[24]{0:T(128)}, u32[]{:S(2)}) copy-start(f32[24]{0:T(128)} %param.19) | copy-start | bytes 292
  217.7 14.3 %copy-start.1 = (f32[4,32,1536]{2,1,0:T(8,128)}, f32[4,32,1536]{2,1,0:T(8,128)S(1)}, u32[]{:S(2)}) copy-start(f32[4,32,1536]{2,1,0:T(8,128)S(1)} %all-to-all-done.5) | copy-start | bytes 2359300
  217.8 13.7 %all-to-all-start.3 = ((f32[4,32,1536]{2,1,0:T(8,128)}), f32[4,32,1536]{2,1,0:T(8,128)S(1)}, u32[]{:S(2)}, u32[]{:S(2)}) async-start(f32[4,32,1536]{2,1,0:T(8,128)} %pad_maximum_fusion), calls=%async_computation.3 | async-start | bytes 1572864 | tf_op jit(solution)/shard_map/all_to_all | solution.py:331
  231.4 0.9 copy-start.2
  274.2 2.1 collective-permute-start.6

commit v2 on v1

v2 whole, which is shorter than its diff:
```python
from functools import partial

import jax
import jax.numpy as jnp
from jax import lax
from jax.experimental import pallas as pl
from jax.experimental.pallas import tpu as pltpu
from jax.sharding import PartitionSpec as P


f32 = jnp.float32
bf16 = jnp.bfloat16
LANES = 128
NEG = -1e30
LOG2E = 1.4426950408889634
LO = 4
SHARES = (4, 4, 4)
TAIL = 1


def split2(x):
    hi = x.astype(bf16)
    return hi, (x - hi.astype(f32)).astype(bf16)


def split3(x):
    hi = x.astype(bf16)
    rest = x - hi.astype(f32)
    mid = rest.astype(bf16)
    return hi, mid, (rest - mid.astype(f32)).astype(bf16)


def mm(a, b):
    return lax.dot_general(a, b, (((1,), (0,)), ((), ())), preferred_element_type=f32)


def mm_nt(a, b):
    return lax.dot_general(a, b, (((1,), (1,)), ((), ())), preferred_element_type=f32)


def iota(shape, dim):
    return lax.broadcasted_iota(jnp.int32, shape, dim)


def params(grid_dims=1):
    return pltpu.CompilerParams(
        dimension_semantics=("arbitrary",) * grid_dims, vmem_limit_bytes=56 * 1024 * 1024
    )


def whole(shape):
    return pl.BlockSpec(shape, lambda *_: (0,) * len(shape))


def dispatch_kernel(
    shift, capacity, split, idx_ref, trow_ref, write_ref, read_ref, logits_ref, oh_ref, ks_ref
):
    rows = trow_ref.shape[1]
    slots = oh_ref.shape[0]
    n = write_ref.shape[1]
    heads = logits_ref.shape[1]
    trow = trow_ref[...]
    owner_row = lax.shift_right_logical(trow, shift)
    local = (trow - lax.shift_left(owner_row, shift)).astype(f32)
    owner_f = jnp.broadcast_to(owner_row.astype(f32), (rows, rows))
    earlier = (owner_f.T == owner_f) & (iota((rows, rows), 0) < iota((rows, rows), 1))
    rank = jnp.sum(jnp.where(earlier, 1.0, 0.0), axis=0, keepdims=True)
    slot = owner_row * capacity + rank.astype(jnp.int32)
    onehot = jnp.where(iota((slots, rows), 0) == slot, 1.0, 0.0).astype(bf16)
    oh_ref[...] = onehot
    high = jnp.floor(local * (1.0 / 16.0))
    sub = iota((LANES, rows), 0)
    marks = jnp.where(
        sub == LANES - 3, high, jnp.where(sub == LANES - 2, local - 16.0 * high, 1.0)
    ).T
    wide = jnp.where(iota((heads, LANES), 0) == iota((heads, LANES), 1), 1.0, 0.0).astype(bf16)
    lane = iota((rows, LANES), 1)
    aux = jnp.where(lane >= LANES - 3, marks, mm(logits_ref[...], wide)).astype(bf16)
    ks_ref[:, :LANES] = mm(onehot, aux).astype(bf16)
    if split:
        key = jnp.where(idx_ref[3] == 0, write_ref[...], read_ref[...])
        ks_ref[:, LANES:] = mm(onehot, key).astype(bf16)
    else:
        ks_ref[:, LANES : LANES + n] = mm(onehot, write_ref[...]).astype(bf16)
        ks_ref[:, LANES + n :] = mm(onehot, read_ref[...]).astype(bf16)


def doc_at(docs_ref, pos):
    start = jnp.int32(0)
    total = pos * 0
    for d in range(docs_ref.shape[0] - 1):
        start = start + docs_ref[d]
        total = total + jnp.where(pos >= start, 1, 0)
    return total


def row_of(ref, c, h):
    return jnp.broadcast_to(ref[c, pl.ds(h, 1), :], (LANES, LANES))


def expand_pair(ref, c, h0):
    upper = iota((LANES, LANES), 0) < LANES // 2
    return jnp.where(upper, row_of(ref, c, h0), row_of(ref, c, h0 + 1)).T


def expand_all(ref, h0):
    return jnp.concatenate([expand_pair(ref, c, h0) for c in range(ref.shape[0])], axis=0)


def setup_kernel(
    heads, split, idx_ref, docs_ref, got_ref, other_ref, heads_ref,
    pm_ref, b_ref, c_ref, bt_ref, ct_ref, dt_ref, sig_ref, at_ref, btt_ref, eat_ref, wt_ref,
    wdt_ref, eadt_ref, mb_ref, skip_ref,
):
    rows = b_ref.shape[0]
    slots = got_ref.shape[0]
    n = b_ref.shape[1]
    chunks = rows // LANES
    p0 = idx_ref[0] * rows
    aux = got_ref[:, :LANES]
    aux_t = aux.astype(f32).T
    pos = aux_t[LANES - 3 : LANES - 2] * 16.0 + aux_t[LANES - 2 : LANES - 1]
    pos = jnp.where(aux_t[LANES - 1 : LANES] > 0.5, pos, -1.0).astype(jnp.int32)
    pm = jnp.where(iota((rows, slots), 0) == pos, 1.0, 0.0).astype(bf16)
    pm_ref[...] = pm
    if split:
        mine = mm(pm, got_ref[:, LANES:])
        other = mm(pm, other_ref[...])
        first = idx_ref[3] == 0
        b_all = jnp.where(first, mine, other)
        c_all = jnp.where(first, other, mine)
    else:
        b_all = mm(pm, got_ref[:, LANES : LANES + n])
        c_all = mm(pm, got_ref[:, LANES + n :])
    b_ref[...] = b_all.astype(bf16)
    c_ref[...] = c_all.astype(bf16)
    logits = jnp.where(iota((rows, LANES), 1) < heads, mm(pm, aux), 0.0)
    x = logits + heads_ref[0:1]
    u = jnp.exp(-jnp.abs(x))
    small = u * (1.0 - u * (0.5 - u * (1.0 / 3.0 - u * (0.25 - u * 0.2))))
    dt = jnp.maximum(x, 0.0) + jnp.where(u < 0.03, small, jnp.log(1.0 + u))
    dt_ref[...] = dt
    sig_ref[...] = jnp.where(x >= 0.0, 1.0, u) / (1.0 + u)
    logdt = jnp.log(dt) * LOG2E
    z = dt * (-jnp.exp(heads_ref[1:2]) * LOG2E)
    tri = jnp.where(iota((LANES, LANES), 0) >= iota((LANES, LANES), 1), 1.0, 0.0).astype(bf16)
    offs = []
    off = jnp.zeros((1, LANES), f32)
    local = []
    for c in range(chunks):
        z0, z1, z2 = split3(z[c * LANES : (c + 1) * LANES])
        a = (mm(tri, z2) + mm(tri, z1)) + mm(tri, z0)
        local.append(a)
        offs.append(off)
        off = off + a[LANES - 1 : LANES]
    doc_before = doc_at(docs_ref, p0 - 1)
    doc_last = doc_at(docs_ref, p0 + rows - 1)
    for c in range(chunks):
        at = slice(c * LANES, (c + 1) * LANES)
        q0 = p0 + c * LANES
        a = local[c]
        ld = logdt[at]
        end = a[LANES - 1 : LANES]
        doc_n = doc_at(docs_ref, q0 + iota((LANES, LANES), 0))
        doc_t = doc_at(docs_ref, q0 + iota((LANES, LANES), 1))
        causal = (doc_n == doc_t) & (iota((LANES, LANES), 0) >= iota((LANES, LANES), 1))
        mb_ref[at] = jnp.where(causal, 0.0, NEG)
        at_ref[c] = a.T
        btt_ref[c] = (a - ld).T
        eat_ref[c] = jnp.where(doc_n == doc_at(docs_ref, q0 - 1), a, NEG).T
        wt_ref[c] = jnp.where(
            doc_n == doc_at(docs_ref, q0 + LANES - 1), end - a + ld, NEG
        ).T
        full = a + offs[c]
        eadt_ref[c] = jnp.where(doc_n == doc_before, full, NEG).T
        wdt_ref[c] = jnp.where(doc_n == doc_last, off - full + ld, NEG).T
        bt_ref[:, at] = b_all[at].T.astype(bf16)
        ct_ref[:, at] = c_all[at].T.astype(bf16)
    width = skip_ref.shape[1]
    to_lanes = jnp.where(
        iota((LANES, width), 0) == lax.shift_right_logical(iota((LANES, width), 1), 6), 1.0, 0.0
    ).astype(bf16)
    s0, s1, s2 = split3(jnp.broadcast_to(heads_ref[2:3], (8, LANES)))
    skip_ref[...] = (mm(s2, to_lanes) + mm(s1, to_lanes)) + mm(s0, to_lanes)


def place_kernel(base, fresh, idx_ref, got_ref, g_ref, pm_ref, wdt_ref, eadt_ref, bt_ref, ct_ref, *refs):
    if not fresh:
        refs = refs[LO:]
    v_ref, outs, (f_ref, u_ref) = refs[0], refs[1 : 1 + LO], refs[1 + LO :]
    rows = v_ref.shape[0]
    v = mm(pm_ref[...], got_ref[...])
    v_ref[...] = v.astype(bf16)
    wide = v.shape[1] // LANES
    h0 = 2 * (base + wide * pl.program_id(0))
    w = jnp.concatenate([expand_all(wdt_ref, h0 + 2 * i) for i in range(wide)], axis=1)
    hi, lo = split2(jnp.exp2(w) * v)
    f_ref[...] = mm(bt_ref[...], hi) + mm(bt_ref[...], lo)
    ea = jnp.concatenate([expand_all(eadt_ref, h0 + 2 * i) for i in range(wide)], axis=1)
    ea = jnp.exp2(ea)
    hi, lo = split2(ea * g_ref[...].astype(f32))
    u_ref[...] = mm(ct_ref[...], hi) + mm(ct_ref[...], lo)
    keep = jnp.broadcast_to(ea[rows - 1 : rows], (8, ea.shape[1]))
    q = f_ref.shape[0] // LO
    for d, ref in enumerate(outs):
        at = pl.multiple_of(lax.bitwise_xor(idx_ref[1], d) * q, q)
        ref[0, :q, :] = f_ref[pl.ds(at, q), :]
        ref[1, :q, :] = u_ref[pl.ds(at, q), :]
        ref[0, q:, :] = keep
        ref[1, q:, :] = keep


def sort_parts(mine, part_refs, sorted_ref):
    for d, ref in enumerate(part_refs):
        sorted_ref[lax.bitwise_xor(mine, d)] = ref[...]


def total_kernel(idx_ref, p0_ref, p1_ref, p2_ref, p3_ref, *refs):
    outs, sorted_ref = refs[:-1], refs[-1]
    q = sorted_ref.shape[2] - 8
    sort_parts(idx_ref[1], (p0_ref, p1_ref, p2_ref, p3_ref), sorted_ref)
    totals = []
    for way in range(2):
        order = list(range(LO))[::-1] if way else list(range(LO))
        state = sorted_ref[order[0], way, :q]
        keep = sorted_ref[order[0], way, q:]
        for k in order[1:]:
            state = sorted_ref[k, way, q : q + 1] * state + sorted_ref[k, way, :q]
            keep = sorted_ref[k, way, q:] * keep
        totals.append((state, keep))
    z = idx_ref[2]
    for e, ref in enumerate(outs, 1):
        up = lax.bitwise_xor(z, e) > z
        ref[:q] = jnp.where(up, totals[0][0], totals[1][0])
        ref[q:] = jnp.where(up, totals[0][1], totals[1][1])


def starts_kernel(lower, others, idx_ref, p0_ref, p1_ref, p2_ref, p3_ref, init_ref, *refs):
    got = refs[:others]
    outs = refs[others : others + LO]
    sorted_ref, far_ref, made_ref = refs[others + LO :]
    q = made_ref.shape[2]
    cols = made_ref.shape[3]
    z = idx_ref[2]
    sort_parts(idx_ref[1], (p0_ref, p1_ref, p2_ref, p3_ref), sorted_ref)
    for e, ref in enumerate(got, 1):
        far_ref[lax.bitwise_xor(z, e)] = ref[...]
    for way in range(2):
        if way:
            acc = jnp.zeros((q, cols), f32)
        else:
            acc = init_ref[:, lower * LANES : lower * LANES + cols]
        planes = list(range(others + 1))
        order = list(range(LO))
        if way:
            planes, order = planes[::-1], order[::-1]
        for p in planes:
            there = (p > z) if way else (p < z)
            acc = jnp.where(there, far_ref[p, q : q + 1] * acc + far_ref[p, :q], acc)
        for k in order:
            made_ref[k, way] = acc
            acc = sorted_ref[k, way, q : q + 1] * acc + sorted_ref[k, way, :q]
    for d, ref in enumerate(outs):
        ref[...] = made_ref[lax.bitwise_xor(idx_ref[1], d)]


def join_quarters(idx_ref, part_refs, way, whole_ref):
    q = part_refs[0].shape[1]
    for d, ref in enumerate(part_refs):
        at = pl.multiple_of(lax.bitwise_xor(idx_ref[1], d) * q, q)
        whole_ref[pl.ds(at, q), :] = ref[way]


def inner_kernel(
    base, v_ref, g_ref, at_ref, btt_ref, b_ref, c_ref, mb_ref,
    yi_ref, dvi_ref, z_ref, cb_ref,
):
    chunks = v_ref.shape[0] // LANES
    half = LANES // 2
    j = pl.program_id(0)
    h0 = 2 * (base + j)

    @pl.when(j == 0)
    def _():
        for c in range(chunks):
            at = slice(c * LANES, (c + 1) * LANES)
            cb_ref[at] = mm_nt(c_ref[at], b_ref[at])
        z_ref[...] = jnp.zeros_like(z_ref)

    low = iota((LANES, LANES), 1) < half
    for c in range(chunks):
        at = slice(c * LANES, (c + 1) * LANES)
        v = v_ref[at]
        g = g_ref[at]
        zero = jnp.zeros_like(v)
        gt = g.astype(f32).T.astype(bf16)
        cb = cb_ref[at]
        mb = mb_ref[at]
        zacc = z_ref[at]
        his, los, dvs = [], [], []
        for k in range(2):
            acol = row_of(at_ref, c, h0 + k).T
            spread = jnp.exp2(acol - row_of(btt_ref, c, h0 + k) + mb)
            mine = low if k == 0 else jnp.logical_not(low)
            gv = mm_nt(jnp.where(mine, g, zero), v)
            zacc = zacc + gv * spread
            hi, lo = split2(cb * spread)
            his.append(hi)
            los.append(lo)
            gk = gt[k * half : (k + 1) * half]
            dvs.append(mm(gk, hi) + mm(gk, lo))
        z_ref[at] = zacc
        dvi_ref[at] = jnp.concatenate(dvs, axis=0).T
        both = jnp.concatenate([jnp.where(low, v, zero), jnp.where(low, zero, v)], axis=0)
        yi_ref[at] = mm(jnp.concatenate(his, axis=1), both) + mm(
            jnp.concatenate(los, axis=1), both
        )


def outer_kernel(
    base, fresh, idx_ref, v_ref, g_ref, yi_ref, dvi_ref, s0_ref, s1_ref, s2_ref, s3_ref,
    eat_ref, wt_ref, b_ref, c_ref, bt_ref, ct_ref, skip_ref, *refs,
):
    if not fresh:
        refs = refs[2:]
    lout_ref, gval_ref, dc_ref, db_ref, gy_ref, vdv_ref, end_ref = refs[:7]
    ea_ref, w_ref, st_ref, ut_ref = refs[7:]
    chunks = v_ref.shape[0] // LANES
    block = v_ref.shape[1]
    wide = block // LANES
    j = pl.program_id(0)
    h0 = 2 * (base + wide * j)

    def factors(ref, c):
        return jnp.exp2(
            jnp.concatenate([expand_pair(ref, c, h0 + 2 * i) for i in range(wide)], axis=1)
        )

    @pl.when(j == 0)
    def _():
        for ref in (dc_ref, db_ref, gy_ref, vdv_ref, end_ref):
            ref[...] = jnp.zeros_like(ref)

    head_of = h0 + lax.shift_right_logical(iota((block, LANES), 0), 6)
    pick = jnp.where(head_of == iota((block, LANES), 1), 1.0, 0.0).astype(bf16)
    skip = skip_ref[0:1]
    join_quarters(idx_ref, (s0_ref, s1_ref, s2_ref, s3_ref), 0, st_ref)
    join_quarters(idx_ref, (s0_ref, s1_ref, s2_ref, s3_ref), 1, ut_ref)
    st = st_ref[...]
    for c in range(chunks):
        at = slice(c * LANES, (c + 1) * LANES)
        vf = v_ref[at].astype(f32)
        gf = g_ref[at].astype(f32)
        ea = factors(eat_ref, c)
        w = factors(wt_ref, c)
        ea_ref[at] = ea
        w_ref[at] = w
        st_hi, st_lo = split2(st)
        y = yi_ref[at] + ea * (mm(c_ref[at], st_hi) + mm(c_ref[at], st_lo))
        lout_ref[at] = (y + skip * vf).astype(bf16)
        p_hi, p_lo = split2(gf * y)
        gy_ref[at] += mm(p_hi, pick) + mm(p_lo, pick)
        eg_hi, eg_lo = split2(ea * gf)
        dc_ref[at] += mm_nt(eg_hi, st_hi) + (mm_nt(eg_hi, st_lo) + mm_nt(eg_lo, st_hi))
        wv_hi, wv_lo = split2(w * vf)
        btc = bt_ref[:, at]
        st = ea[LANES - 1 : LANES] * st + (mm(btc, wv_hi) + mm(btc, wv_lo))
    ut = ut_ref[...]
    final = jnp.sum(st * ut, axis=0, keepdims=True)
    e0, e1, e2 = split3(jnp.broadcast_to(final, (8, block)))
    end_ref[...] += (mm(e2, pick) + mm(e1, pick)) + mm(e0, pick)
    for c in reversed(range(chunks)):
        at = slice(c * LANES, (c + 1) * LANES)
        vf = v_ref[at].astype(f32)
        gf = g_ref[at].astype(f32)
        ea = ea_ref[at]
        w = w_ref[at]
        ut_hi, ut_lo = split2(ut)
        dv = dvi_ref[at] + w * (mm(b_ref[at], ut_hi) + mm(b_ref[at], ut_lo))
        gval_ref[at] = (dv + skip * gf).astype(bf16)
        p_hi, p_lo = split2(vf * dv)
        vdv_ref[at] += mm(p_hi, pick) + mm(p_lo, pick)
        wv_hi, wv_lo = split2(w * vf)
        db_ref[at] += mm_nt(wv_hi, ut_hi) + (mm_nt(wv_hi, ut_lo) + mm_nt(wv_lo, ut_hi))
        eg_hi, eg_lo = split2(ea * gf)
        ctc = ct_ref[:, at]
        ut = ea[LANES - 1 : LANES] * ut + (mm(ctc, eg_hi) + mm(ctc, eg_lo))


def finish_kernel(inner, outer, *refs):
    zs = refs[:inner]
    parts = [refs[inner + 5 * i : inner + 5 * i + 5] for i in range(outer)]
    b_ref, c_ref, dt_ref, sig_ref, heads_ref, glog_ref, keys_ref = refs[inner + 5 * outer :]
    rows = b_ref.shape[0]
    n = b_ref.shape[1]
    heads = glog_ref.shape[1]

    def total(i, at):
        out = parts[0][i][at]
        for part in parts[1:]:
            out = out + part[i][at]
        return out

    rate = -jnp.exp(heads_ref[1:2])
    tri = jnp.where(iota((LANES, LANES), 0) <= iota((LANES, LANES), 1), 1.0, 0.0).astype(bf16)
    off = total(4, slice(0, 1))
    for c in reversed(range(rows // LANES)):
        at = slice(c * LANES, (c + 1) * LANES)
        vdv = total(3, at)
        q0, q1, q2 = split3(total(2, at) - vdv)
        run = (mm(tri, q2) + mm(tri, q1)) + mm(tri, q0) + off
        off = run[0:1]
        glog = (vdv / dt_ref[at] + rate * run) * sig_ref[at]
        glog_ref[at] = glog[:, :heads]
        z = zs[0][at]
        for ref in zs[1:]:
            z = z + ref[at]
        z_hi, z_lo = split2(z)
        t_hi, t_lo = split2(z.T)
        keys_ref[at, n:] = total(0, at) + (mm(z_hi, b_ref[at]) + mm(z_lo, b_ref[at]))
        keys_ref[at, :n] = total(1, at) + (mm(t_hi, c_ref[at]) + mm(t_lo, c_ref[at]))


def in_group(size, d):
    return [(i, i - i % LO + ((i % LO) ^ d)) for i in range(size)]


def body(
    token_values, step_logits, write_keys, read_queries, target, doc_lengths,
    decay_log, step_bias, skip_gain, init_state, out_grad,
):
    rows = token_values.shape[0]
    size = lax.axis_size("seq")
    me = lax.axis_index("seq")
    heads = decay_log.shape[0]
    width = token_values.shape[1]
    head_width = width // heads
    n = write_keys.shape[1]
    capacity = 2 * rows // size
    slots = size * capacity
    pairs = width // LANES
    assert head_width * 2 == LANES and n == LANES and heads <= LANES - 3
    assert rows & (rows - 1) == 0 and rows % LANES == 0 and size % LO == 0
    hi_count = size // LO
    others = hi_count - 1
    q = n // LO
    chunks = rows // LANES
    vmem = pltpu.CompilerParams(vmem_limit_bytes=56 * 1024 * 1024)

    def sds(shape, dtype=f32):
        return jax.ShapeDtypeStruct(shape, dtype)

    split = lax.axis_size("head") == 2
    kw = LANES + (n if split else 2 * n)
    idx = jnp.stack([me, me % LO, me // LO, lax.axis_index("head")]).astype(jnp.int32)
    smem = pl.BlockSpec(memory_space=pltpu.SMEM)
    anywhere = pl.BlockSpec(memory_space=pl.ANY)
    full = pl.BlockSpec(memory_space=pltpu.VMEM)
    tiles = whole((chunks, LANES, LANES))
    tile_shape = sds((chunks, LANES, LANES))

    onehot, kslots = pl.pallas_call(
        partial(dispatch_kernel, rows.bit_length() - 1, capacity, split),
        in_specs=[smem, full, full, full, full],
        out_shape=(sds((slots, rows), bf16), sds((slots, kw), bf16)),
        compiler_params=vmem,
        name="dispatch",
    )(idx, target.reshape(1, rows), write_keys, read_queries, step_logits)

    def route(x):
        there = x.reshape(size, capacity, x.shape[1])
        there = lax.all_to_all(there, "seq", split_axis=0, concat_axis=0, tiled=True)
        return there.reshape(slots, x.shape[1])

    got_keys = route(kslots)
    spans = make_plan(pairs)
    sent = []
    for lower, upper in spans:
        part = token_values[:, lower * LANES : upper * LANES]
        sent.append(jnp.dot(onehot, part, preferred_element_type=f32).astype(bf16))
    got_values = [route(part) for part in sent]

    per_head = jnp.pad(
        jnp.stack([step_bias, decay_log, skip_gain]), ((0, 5), (0, LANES - heads))
    )
    if split:
        other = lax.ppermute(got_keys[:, LANES:], "head", [(0, 1), (1, 0)])
    else:
        other = got_keys
    (
        pm, b, c, bt, ct, dt, sig, at, btt, eat, wt, wdt, eadt, mb, skip_row
    ) = pl.pallas_call(
        partial(setup_kernel, heads, split),
        in_specs=[smem, smem, full, full, full],
        out_shape=[
            sds((rows, slots), bf16),
            sds((rows, n), bf16), sds((rows, n), bf16),
            sds((n, rows), bf16), sds((n, rows), bf16),
            sds((rows, LANES)), sds((rows, LANES)),
            *[tile_shape] * 6,
            sds((rows, LANES)),
            sds((8, width)),
        ],
        compiler_params=vmem,
        name="setup",
    )(idx, doc_lengths, got_keys, other, per_head)

    init_part = lax.dynamic_slice_in_dim(init_state, (me % LO) * q, q, axis=2)
    init_part = init_part.reshape(width, q).T

    def ring(parts):
        out = [parts[0]]
        for d in range(1, LO):
            out.append(lax.ppermute(parts[d], "seq", in_group(size, d)))
        return out

    def exchange(parts, lower):
        cols = parts[0].shape[2]
        got = ring(parts)
        mine = pl.pallas_call(
            total_kernel,
            in_specs=[smem, *[full] * LO],
            out_shape=[sds((q + 8, cols))] * others,
            scratch_shapes=[pltpu.VMEM((LO, 2, q + 8, cols), f32)],
            compiler_params=vmem,
        )(idx, *got)
        far = []
        for e in range(1, hi_count):
            perm = [(i, ((i // LO) ^ e) * LO + i % LO) for i in range(size)]
            far.append(lax.ppermute(mine[e - 1], "seq", perm))
        starts = pl.pallas_call(
            partial(starts_kernel, lower, others),
            in_specs=[smem, *[full] * (LO + 1 + others)],
            out_shape=[sds((2, q, cols))] * LO,
            scratch_shapes=[
                pltpu.VMEM((LO, 2, q + 8, cols), f32),
                pltpu.VMEM((hi_count, q + 8, cols), f32),
                pltpu.VMEM((LO, 2, q, cols), f32),
            ],
            compiler_params=vmem,
        )(idx, *got, init_part, *far)
        return ring(starts)

    def blocking(lower, upper):
        many = 2 if (upper - lower) % 2 == 0 and lower % 2 == 0 else 1
        return many, many * LANES, (upper - lower) // many

    cut = max(len(spans) - TAIL, 0)
    teams = [t for t in (list(range(cut)), list(range(cut, len(spans)))) if t]
    placed = []
    zs = []
    inners = []
    payloads = {}
    for t, team in enumerate(teams):
        first, stop = spans[team[0]][0], spans[team[-1]][1]
        payload = None
        for i in team:
            lower, upper = spans[i]
            cols = (upper - lower) * LANES
            many, block, steps = blocking(lower, upper)
            inside = (lower - first) // many
            fresh = payload is None
            v, *payload = pl.pallas_call(
                partial(place_kernel, lower, fresh),
                grid=(steps,),
                in_specs=[
                    smem,
                    pl.BlockSpec((slots, block), lambda j: (0, j)),
                    pl.BlockSpec((rows, block), lambda j, o=lower // many: (0, o + j)),
                    whole((rows, slots)),
                    tiles, tiles, whole((n, rows)), whole((n, rows)),
                    *([] if fresh else [anywhere] * LO),
                ],
                out_specs=[
                    pl.BlockSpec((rows, block), lambda j: (0, j)),
                    *[pl.BlockSpec((2, q + 8, block), lambda j, o=inside: (0, 0, o + j))] * LO,
                ],
                out_shape=[
                    sds((rows, cols), bf16), *[sds((2, q + 8, (stop - first) * LANES))] * LO
                ],
                scratch_shapes=[pltpu.VMEM((n, block), f32)] * 2,
                input_output_aliases={} if fresh else {8 + d: 1 + d for d in range(LO)},
                compiler_params=params(),
            )(idx, got_values[i], out_grad, pm, wdt, eadt, bt, ct, *(payload or []))
            placed.append(v)
            col = pl.BlockSpec((rows, LANES), lambda j: (0, j))
            yi, dvi, z = pl.pallas_call(
                partial(inner_kernel, lower),
                grid=(upper - lower,),
                in_specs=[
                    col,
                    pl.BlockSpec((rows, LANES), lambda j, o=lower: (0, o + j)),
                    tiles, tiles, whole((rows, n)), whole((rows, n)), whole((rows, LANES)),
                ],
                out_specs=[col, col, whole((rows, LANES))],
                out_shape=[sds((rows, cols)), sds((rows, cols)), sds((rows, LANES))],
                scratch_shapes=[pltpu.VMEM((rows, LANES), f32)],
                compiler_params=params(),
            )(v, out_grad, at, btt, b, c, mb)
            inners.append((yi, dvi))
            zs.append(z)
        payloads[t] = (payload, first)

    states = {}
    for t, team in enumerate(teams):
        payload, first = payloads[t]
        st = exchange(payload, first)
        for i in team:
            states[i] = (st, first)

    partials = []
    made = None
    for i, (lower, upper) in enumerate(spans):
        cols = (upper - lower) * LANES
        many, block, steps = blocking(lower, upper)
        st, first = states[i]
        inside = (lower - first) // many
        acc = whole((rows, LANES))
        own = pl.BlockSpec((rows, block), lambda j: (0, j))
        shifted = pl.BlockSpec((rows, block), lambda j, o=lower // many: (0, o + j))
        res = pl.pallas_call(
            partial(outer_kernel, lower, made is None),
            grid=(steps,),
            in_specs=[
                smem, own, shifted, own, own,
                *[pl.BlockSpec((2, q, block), lambda j, o=inside: (0, 0, o + j))] * LO,
                tiles, tiles,
                whole((rows, n)), whole((rows, n)), whole((n, rows)), whole((n, rows)),
                pl.BlockSpec((8, block), lambda j, o=lower // many: (0, o + j)),
                *([] if made is None else [anywhere] * 2),
            ],
            out_specs=[shifted, shifted, acc, acc, acc, acc, whole((8, LANES))],
            out_shape=[
                sds((rows, width), bf16), sds((rows, width), bf16),
                *[sds((rows, LANES))] * 4, sds((8, LANES)),
            ],
            scratch_shapes=[
                pltpu.VMEM((rows, block), f32), pltpu.VMEM((rows, block), f32),
                pltpu.VMEM((n, block), f32), pltpu.VMEM((n, block), f32),
            ],
            input_output_aliases={} if made is None else {16: 0, 17: 1},
            compiler_params=params(),
        )(
            idx, placed[i], out_grad, *inners[i], *st, eat, wt, b, c, bt, ct, skip_row,
            *(made or ()),
        )
        made = (res[0], res[1])
        partials.extend(res[2:])

    grad_logits, keys_grad = pl.pallas_call(
        partial(finish_kernel, len(zs), len(spans)),
        out_shape=[sds((rows, heads)), sds((rows, 2 * n))],
        compiler_params=vmem,
        name="finish",
    )(*zs, *partials, b, c, dt, sig, per_head)
    if split:
        keys_grad = keys_grad + lax.ppermute(keys_grad, "head", [(0, 1), (1, 0)])
    else:
        keys_grad = lax.psum(keys_grad, "head")
    return made[0], made[1], grad_logits, keys_grad[:, :n], keys_grad[:, n:]


def make_plan(pairs):
    total = sum(SHARES)
    edges = [0]
    for share in SHARES:
        edges.append(edges[-1] + share)
    cuts = [pairs * e // total for e in edges]
    return [(a, b) for a, b in zip(cuts[:-1], cuts[1:]) if b > a]


def solution(mesh):
    return jax.shard_map(
        body,
        mesh=mesh,
        in_specs=(
            P("seq", "head"),
            P("seq", "head"),
            P("seq", None),
            P("seq", None),
            P("seq"),
            P(),
            P("head"),
            P("head"),
            P("head"),
            P("head", None, None),
            P("seq", "head"),
        ),
        out_specs=(
            P("seq", "head"),
            P("seq", "head"),
            P("seq", "head"),
            P("seq", None),
            P("seq", None),
        ),
        check_vma=False,
    )
```

time: 283 us -> 234 us (0.83); the launches traced: 278 us -> 233 us
  waiting for transfers between devices: 131 us -> 79.1 us
  Pallas kernels: 69.3 us -> 82.3 us
  other arithmetic: 11.5 us -> 2.26 us
  local copies, waits for them, and re-layouts: 18.1 us -> 12.3 us
  starting transfers between devices: 43.2 us -> 47.5 us
  matrix products: 4.69 us -> 8.85 us
    ppermute x6 -> x19, waiting for transfers between devices: 86.1 us -> 25.8 us  [the longest x12 16.8 us: ring(): out.append(lax.ppermute(parts[d], 'seq', in_group(size, d)))]
    pallas_call x5 -> x16, Pallas kernels: 69.3 us -> 82.3 us  [the longest x3 31.3 us: body(): pl.pallas_call(partial(outer_kernel, lower, made is None), grid=(steps,),...]
    all_to_all x6 -> x4, waiting for transfers between devices: 43.9 us -> 52.9 us  [route(): lax.all_to_all(there, 'seq', split_axis=0, concat_axis=0, tiled=True)]
    ppermute x6 -> x19, starting transfers between devices: 14.8 us -> 23.3 us  [the longest x12 13.9 us: ring(): out.append(lax.ppermute(parts[d], 'seq', in_group(size, d)))]
    another operation x7 -> x2, other arithmetic: 7.46 us -> 1.15 us  [the longest x1 0.59 us: body(): jnp.stack([step_bias, decay_log, skip_gain])]
    unnamed x30 -> x58, local copies, waits for them, and re-layouts: 4.44 us -> 10.3 us
    slice x8 -> x2, local copies, waits for them, and re-layouts: 6.22 us -> 0.84 us  [the longest x1 0.82 us: body(): return (made[0], made[1], grad_logits, keys_grad[:, :n], keys_grad[:, n:])]
    dot_general x1 -> x3, matrix products: 4.69 us -> 8.85 us  [body(): sent.append(jnp.dot(onehot, part, preferred_element_type=f32).astype(bf16))]
  transfers between devices with their start and end apart: 13 -> 24, of which waited for: 7 -> 11; matrix products, arithmetic and copies ran while one was open for 8% -> 5% of each run, Pallas kernels for 0% -> 28%
where the time goes in v2:
time: 234 us; the launch traced here: 233 us
  Pallas kernels  82.3 us (35%)
  waiting for transfers between devices  79.1 us (34%)
  starting transfers between devices  47.5 us (20%)
  local copies, waits for them, and re-layouts  12.3 us (5%)
  matrix products  8.85 us (4%)
    all_to_all x4, waiting for transfers between devices, route(): lax.all_to_all(there, 'seq', split_axis=0, concat_axis=0, tiled=True)  52.9 us
    pallas_call x3, Pallas kernels, body(): pl.pallas_call(partial(outer_kernel, lower, made is None), grid=(steps,),...  31.3 us
    all_to_all x4, starting transfers between devices, route(): lax.all_to_all(there, 'seq', split_axis=0, concat_axis=0, tiled=True)  24.2 us
    pallas_call x3, Pallas kernels, body(): pl.pallas_call(partial(inner_kernel, lower), grid=(upper - lower,), in_sp...  17 us
    ppermute x12, waiting for transfers between devices, ring(): out.append(lax.ppermute(parts[d], 'seq', in_group(size, d)))  16.8 us
    ppermute x12, starting transfers between devices, ring(): out.append(lax.ppermute(parts[d], 'seq', in_group(size, d)))  13.9 us
    pallas_call x3, Pallas kernels, body(): pl.pallas_call(partial(place_kernel, lower, fresh), grid=(steps,), in_spe...  13.2 us
    unnamed x58, local copies, waits for them, and re-layouts  10.3 us
  transfers between devices with their start and end apart: 24, of which 11 were waited for; matrix products, arithmetic and copies ran while one was open for 5% of the time, Pallas kernels for 28%

profile of v2, /device:TPU:0, one launch (start us, length us, event | category | flops | bytes accessed | tf_op | source)
XLA Modules:
  0.0 233.3 jit_solution(8305021879637953544)
XLA Ops:
  0.7 1.6 copy.24.logits_ref
  2.2 0.6 pad_add_fusion.idx_ref
  2.8 2.9 %dispatch.1 = (bf16[1024,512]{1,0:T(8,128)(2,1)}, bf16[1024,256]{1,0:T(8,128)(2,1)}) custom-call(s32[4]{0:T(128)} %pad_add_fusion.idx_ref, s32[1,512]{1,0:T(1,128)} %bitcast.32, bf16[512,128]{1,0:T(8,128)(2,1)} %write_ref.1, bf16[512,128]{1,0:T(8,128)(2,1)} %read_ref.1, bf16[512,24]{1,0:T(8,128)(2,1)} %copy.24.logits_ref), custom_call_target="tpu_custom_call" | custom-call | tf_op jit(solution)/shard_map/dispatch/pallas_call | solution.py:462
  5.7 8.3 %all-to-all-start.1 = ((bf16[16,64,256]{2,1,0:T(8,128)(2,1)}), bf16[16,64,256]{2,1,0:T(8,128)(2,1)S(1)}, u32[]{:S(2)}, u32[]{:S(2)}) async-start(bf16[16,64,256]{2,1,0:T(8,128)(2,1)} %bitcast.31), calls=%async_computation.1 | async-start | bytes 1048576 | tf_op jit(solution)/shard_map/all_to_all | solution.py:472
  14.1 3.0 %convolution_convert_fusion = bf16[1024,512]{1,0:T(8,128)(2,1)} fusion(bf16[1024,512]{1,0:T(8,128)(2,1)} %get-tuple-element.83, bf16[512,1536]{1,0:T(8,128)(2,1)} %param.11), kind=kOutput, calls=%fused_computation | convolution fusion | flops 537395200 | bytes 2621440 | tf_op jit(solution)/shard_map/dot_general | solution.py:480
  17.1 12.0 %all-to-all-done.1 = bf16[16,64,256]{2,1,0:T(8,128)(2,1)S(1)} async-done(((bf16[16,64,256]{2,1,0:T(8,128)(2,1)}), bf16[16,64,256]{2,1,0:T(8,128)(2,1)S(1)}, u32[]{:S(2)}, u32[]{:S(2)}) %all-to-all-start.1) | async-done | bytes 524320 | tf_op jit(solution)/shard_map/all_to_all | solution.py:472
  29.2 3.9 %all-to-all-start.3 = ((bf16[16,64,512]{2,1,0:T(8,128)(2,1)}), bf16[16,64,512]{2,1,0:T(8,128)(2,1)S(1)}, u32[]{:S(2)}, u32[]{:S(2)}) async-start(bf16[16,64,512]{2,1,0:T(8,128)(2,1)} %bitcast.16), calls=%async_computation.3 | async-start | bytes 2097152 | tf_op jit(solution)/shard_map/all_to_all | solution.py:472
  33.1 2.8 %convolution_convert_fusion.1 = bf16[1024,512]{1,0:T(8,128)(2,1)} fusion(bf16[1024,512]{1,0:T(8,128)(2,1)S(1)} %copy-done.27, bf16[512,1536]{1,0:T(8,128)(2,1)} %param.11), kind=kOutput, calls=%fused_computation.1 | convolution fusion | flops 537395200 | bytes 2621440 | tf_op jit(solution)/shard_map/dot_general | solution.py:480
  35.9 20.9 %all-to-all-done.3 = bf16[16,64,512]{2,1,0:T(8,128)(2,1)S(1)} async-done(((bf16[16,64,512]{2,1,0:T(8,128)(2,1)}), bf16[16,64,512]{2,1,0:T(8,128)(2,1)S(1)}, u32[]{:S(2)}, u32[]{:S(2)}) %all-to-all-start.3) | async-done | bytes 1048608 | tf_op jit(solution)/shard_map/all_to_all | solution.py:472
  56.8 5.9 %all-to-all-start.2 = ((bf16[16,64,512]{2,1,0:T(8,128)(2,1)}), bf16[16,64,512]{2,1,0:T(8,128)(2,1)S(1)}, u32[]{:S(2)}, u32[]{:S(2)}) async-start(bf16[16,64,512]{2,1,0:T(8,128)(2,1)} %bitcast.30), calls=%async_computation.2 | async-start | bytes 2097152 | tf_op jit(solution)/shard_map/all_to_all | solution.py:472
  62.7 3.0 %convolution_convert_fusion.2 = bf16[1024,512]{1,0:T(8,128)(2,1)} fusion(bf16[1024,512]{1,0:T(8,128)(2,1)} %get-tuple-element.83, bf16[512,1536]{1,0:T(8,128)(2,1)} %param.11), kind=kOutput, calls=%fused_computation.2 | convolution fusion | flops 537395200 | bytes 2621440 | tf_op jit(solution)/shard_map/dot_general | solution.py:480
  65.7 19.9 %all-to-all-done.2 = bf16[16,64,512]{2,1,0:T(8,128)(2,1)S(1)} async-done(((bf16[16,64,512]{2,1,0:T(8,128)(2,1)}), bf16[16,64,512]{2,1,0:T(8,128)(2,1)S(1)}, u32[]{:S(2)}, u32[]{:S(2)}) %all-to-all-start.2) | async-done | bytes 1048608 | tf_op jit(solution)/shard_map/all_to_all | solution.py:472
  85.6 1.0 copy-done.3
  86.6 6.0 %all-to-all-start = ((bf16[16,64,512]{2,1,0:T(8,128)(2,1)}), bf16[16,64,512]{2,1,0:T(8,128)(2,1)S(1)}, u32[]{:S(2)}, u32[]{:S(2)}) async-start(bf16[16,64,512]{2,1,0:T(8,128)(2,1)} %bitcast.29), calls=%async_computation | async-start | bytes 2097152 | tf_op jit(solution)/shard_map/all_to_all | solution.py:472
  92.8 0.6 select_maximum_fusion.heads_ref.refs_22_
  93.4 0.9 collective-permute-done.other_ref
  94.3 0.7 copy-done.14
  95.0 5.0 %setup.1 = (bf16[512,1024]{1,0:T(8,128)(2,1)}, bf16[512,128]{1,0:T(8,128)(2,1)}, bf16[512,128]{1,0:T(8,128)(2,1)}, bf16[128,512]{1,0:T(8,128)(2,1)}, bf16[128,51...) custom-call(s32[4]{0:T(128)} %pad_add_fusion.idx_ref, ...), custom_call_target="tpu_custom_call" | custom-call | tf_op jit(solution)/shard_map/setup/pallas_call | solution.py:492
  100.0 4.4 %shard_map.150 = (bf16[512,512]{1,0:T(8,128)(2,1)}, f32[2,40,1024]{2,1,0:T(8,128)}, f32[2,40,1024]{2,1,0:T(8,128)}, f32[2,40,1024]{2,1,0:T(8,128)}, f32[2,40,1024]{2,1,0:T(8,128)}) custom-call(s32[4]{0:T(128)} %pad_add_fusion.idx_ref, bf16[1024,512]{1,0:T(8,128)(2,1)} %bitcast.22, bf16[512,1536]{1,0:T(8,128)(2,1)} %g_ref.17, ...), custom_call_target="tpu_custom_call" | custom-call | tf_op jit(solution)/shard_map/pallas_call | solution.py:563
  104.4 4.4 %shard_map.151 = (bf16[512,512]{1,0:T(8,128)(2,1)}, f32[2,40,1024]{2,1,0:T(8,128)}, f32[2,40,1024]{2,1,0:T(8,128)}, f32[2,40,1024]{2,1,0:T(8,128)}, f32[2,40,1024]{2,1,0:T(8,128)}) custom-call(s32[4]{0:T(128)} %pad_add_fusion.idx_ref, bf16[1024,512]{1,0:T(8,128)(2,1)} %bitcast.23, ...), custom_call_target="tpu_custom_call", output_to_operand_aliasing={{1}: (8, {}), {2}: (9, {}), {3}: (10, {}), {4}: (11, {})} | custom-call | tf_op jit(solution)/shard_map/pallas_call | solution.py:563
  108.8 2.0 collective-permute-start.10
  110.8 1.5 collective-permute-start.11
  112.4 9.4 %collective-permute-done.10.p1_ref = f32[2,40,1024]{2,1,0:T(8,128)S(1)} collective-permute-done((f32[2,40,1024]{2,1,0:T(8,128)}, f32[2,40,1024]{2,1,0:T(8,128)S(1)}, u32[]{:S(2)}, u32[]{:S(2)}) %collective-permute-start.10) | collective-permute-done | bytes 327712 | tf_op jit(solution)/shard_map/ppermute | solution.py:514
  121.7 7.4 %collective-permute-done.12.p3_ref = f32[2,40,1024]{2,1,0:T(8,128)S(1)} collective-permute-done((f32[2,40,1024]{2,1,0:T(8,128)}, f32[2,40,1024]{2,1,0:T(8,128)S(1)}, u32[]{:S(2)}, u32[]{:S(2)}) %collective-permute-start.12) | collective-permute-done | bytes 327712 | tf_op jit(solution)/shard_map/ppermute | solution.py:514
  129.1 0.7 copy-done.7
  129.9 2.2 shard_map.153
  132.1 2.3 collective-permute-start.13
  134.4 1.9 collective-permute-start.14
  136.3 0.5 collective-permute-start.15
  136.8 1.0 copy-done.1
  137.8 4.4 %shard_map.146 = (bf16[512,512]{1,0:T(8,128)(2,1)}, f32[2,40,512]{2,1,0:T(8,128)}, f32[2,40,512]{2,1,0:T(8,128)}, f32[2,40,512]{2,1,0:T(8,128)}, f32[2,40,512]{2,1,0:T(8,128)}) custom-call(s32[4]{0:T(128)} %pad_add_fusion.idx_ref, bf16[1024,512]{1,0:T(8,128)(2,1)} %bitcast.21, bf16[512,1536]{1,0:T(8,128)(2,1)} %g_ref.17, ...), custom_call_target="tpu_custom_call" | custom-call | tf_op jit(solution)/shard_map/pallas_call | solution.py:563
  142.1 1.5 collective-permute-start.1
  143.7 0.5 collective-permute-start.2
  144.2 1.5 collective-permute-start.3
  145.9 0.9 copy.27
  146.9 2.6 %collective-permute-done.14.refs_1_ = f32[40,1024]{1,0:T(8,128)S(1)} collective-permute-done((f32[40,1024]{1,0:T(8,128)}, f32[40,1024]{1,0:T(8,128)S(1)}, u32[]{:S(2)}, u32[]{:S(2)}) %collective-permute-start.14) | collective-permute-done | bytes 163872 | tf_op jit(solution)/shard_map/ppermute | solution.py:530
  149.4 0.6 copy-done.16
  150.1 2.8 %shard_map.154 = (f32[2,32,1024]{2,1,0:T(8,128)}, f32[2,32,1024]{2,1,0:T(8,128)}, f32[2,32,1024]{2,1,0:T(8,128)}, f32[2,32,1024]{2,1,0:T(8,128)}) custom-call(s32[4]{0:T(128)} %pad_add_fusion.idx_ref, f32[2,40,1024]{2,1,0:T(8,128)} %get-tuple-element.119.p0_ref, f32[2,40,1024]{2,1,0:T(8,128)} %copy-done.5, f32[2,40,1024]{2,1,0:T(8,128)} %copy-done.6, ...), custom_call_target="tpu_custom_call" | custom-call | tf_op jit(solution)/shard_map/pallas_call | solution.py:531
  152.9 1.6 collective-permute-start.16
  154.6 0.6 copy-done.11
  155.4 2.0 shard_map.148
  157.3 2.6 %collective-permute-start.4 = (f32[40,512]{1,0:T(8,128)}, f32[40,512]{1,0:T(8,128)S(1)}, u32[]{:S(2)}, u32[]{:S(2)}) collective-permute-start(f32[40,512]{1,0:T(8,128)} %get-tuple-element.102), channel_id=1, source_target_pairs={{0,8},{2,10},{4,12},{6,14},{8,0},{10,2},{12,4},{14,6},{16,24},{18,... | collective-permute-start | bytes 245768 | tf_op jit(solution)/shard_map/ppermute | solution.py:530
  160.4 1.1 collective-permute-start.18
  161.5 0.6 collective-permute-start.5
  162.5 1.5 collective-permute-start.6
  164.0 3.9 %collective-permute-done.5.refs_1_ = f32[40,512]{1,0:T(8,128)S(1)} collective-permute-done((f32[40,512]{1,0:T(8,128)}, f32[40,512]{1,0:T(8,128)S(1)}, u32[]{:S(2)}, u32[]{:S(2)}) %collective-permute-start.5) | collective-permute-done | bytes 81952 | tf_op jit(solution)/shard_map/ppermute | solution.py:530
  167.9 1.2 collective-permute-done.6.refs_2_
  169.1 0.6 copy-done.23
  169.7 2.3 shard_map.149
  172.1 2.2 collective-permute-start.7
  174.2 0.6 collective-permute-start.8
  174.8 0.9 collective-permute-start.9
  175.7 5.6 %shard_map.152 = (f32[512,512]{1,0:T(8,128)}, f32[512,512]{1,0:T(8,128)}, f32[512,128]{1,0:T(8,128)}) custom-call(bf16[512,512]{1,0:T(8,128)(2,1)} %get-tuple-element.116.v_ref, bf16[512,1536]{1,0:T(8,128)(2,1)} %g_ref.17, f32[4,128,128]{2,1,0:T(8,128)} %get-tuple-element.91.at_ref, f32[4,128,128]{2,1,0:T(8,128)} %get-tuple-element.92.btt_ref, ...), custom_call_target="tpu_custom_call" | custom-call | tf_op jit(solution)/shard_map/pallas_call | solution.py:587
  181.4 5.7 %shard_map.155 = (f32[512,512]{1,0:T(8,128)}, f32[512,512]{1,0:T(8,128)}, f32[512,128]{1,0:T(8,128)}) custom-call(bf16[512,512]{1,0:T(8,128)(2,1)} %get-tuple-element.130.v_ref, bf16[512,1536]{1,0:T(8,128)(2,1)} %g_ref.17, f32[4,128,128]{2,1,0:T(8,128)} %get-tuple-element.91.at_ref, f32[4,128,128]{2,1,0:T(8,128)} %get-tuple-element.92.btt_ref, ...), custom_call_target="tpu_custom_call" | custom-call | tf_op jit(solution)/shard_map/pallas_call | solution.py:587
  187.0 5.7 %shard_map.147 = (f32[512,512]{1,0:T(8,128)}, f32[512,512]{1,0:T(8,128)}, f32[512,128]{1,0:T(8,128)}) custom-call(bf16[512,512]{1,0:T(8,128)(2,1)} %get-tuple-element.90.v_ref, bf16[512,1536]{1,0:T(8,128)(2,1)} %g_ref.17, f32[4,128,128]{2,1,0:T(8,128)} %get-tuple-element.91.at_ref, f32[4,128,128]{2,1,0:T(8,128)} %get-tuple-element.92.btt_ref, ...), custom_call_target="tpu_custom_call" | custom-call | tf_op jit(solution)/shard_map/pallas_call | solution.py:587
  192.7 0.7 copy-done.9
  193.5 10.5 %shard_map.156 = (bf16[512,1536]{1,0:T(8,128)(2,1)}, bf16[512,1536]{1,0:T(8,128)(2,1)}, f32[512,128]{1,0:T(8,128)}, f32[512,128]{1,0:T(8,128)}, f32[512,128]{1,0...) custom-call(s32[4]{0:T(128)} %pad_add_fusion.idx_ref, bf16[512,512]{1,0:T(8,128)(2,1)} %get-tuple-element.130.v_ref, ...), custom_call_target="tpu_custom_call" | custom-call | tf_op jit(solution)/shard_map/pallas_call | solution.py:621
  204.0 10.4 %shard_map.157 = (bf16[512,1536]{1,0:T(8,128)(2,1)}, bf16[512,1536]{1,0:T(8,128)(2,1)}, f32[512,128]{1,0:T(8,128)}, f32[512,128]{1,0:T(8,128)}, f32[512,128]{1,0...) custom-call(s32[4]{0:T(128)} %pad_add_fusion.idx_ref, ...), custom_call_target="tpu_custom_call", output_to_operand_aliasing={{0}: (16, {}), {1}: (17, {})} | custom-call | tf_op jit(solution)/shard_map/pallas_call | solution.py:621
  214.5 0.6 copy-done.18
  215.2 10.4 %shard_map.158 = (bf16[512,1536]{1,0:T(8,128)(2,1)}, bf16[512,1536]{1,0:T(8,128)(2,1)}, f32[512,128]{1,0:T(8,128)}, f32[512,128]{1,0:T(8,128)}, f32[512,128]{1,0...) custom-call(s32[4]{0:T(128)} %pad_add_fusion.idx_ref, ...), custom_call_target="tpu_custom_call", output_to_operand_aliasing={{0}: (16, {}), {1}: (17, {})} | custom-call | tf_op jit(solution)/shard_map/pallas_call | solution.py:621
  225.6 3.6 %finish.1 = (f32[512,24]{1,0:T(8,128)}, f32[512,256]{1,0:T(8,128)}) custom-call(f32[512,128]{1,0:T(8,128)} %get-tuple-element.139.refs_0_, f32[512,128]{1,0:T(8,128)} %get-tuple-element.140.refs_1_, f32[512,128]{1,0:T(8,128)} %get-tuple-element.141.refs_2_, f32[512,128]{1,0:T(8,128)} %get-tuple-element.142.refs_3_, f32[512,128]{1,0:T(8,128)} %get-tuple-element.143.refs_4_, ...), custom_call_target="tpu_custom_call" | custom-call | tf_op jit(solution)/shard_map/finish/pallas_call | solution.py:650
  229.2 1.7 copy.26
  231.3 1.1 add.16
  232.5 0.8 fusion.3
  (68 shorter events, 2.3 us)
Async XLA Ops:
  0.6 145.0 %copy-start = (f32[24,64,128]{2,1,0:T(8,128)S(1)}, f32[24,64,128]{2,1,0:T(8,128)}, u32[]{:S(2)}) copy-start(f32[24,64,128]{2,1,0:T(8,128)} %param.20) | copy-start | bytes 2359300
  5.7 23.4 %all-to-all-start.1 = ((bf16[16,64,256]{2,1,0:T(8,128)(2,1)}), bf16[16,64,256]{2,1,0:T(8,128)(2,1)S(1)}, u32[]{:S(2)}, u32[]{:S(2)}) async-start(bf16[16,64,256]{2,1,0:T(8,128)(2,1)} %bitcast.31), calls=%async_computation.1 | async-start | bytes 1048576 | tf_op jit(solution)/shard_map/all_to_all | solution.py:472
  17.1 16.0 %copy-start.27 = (bf16[1024,512]{1,0:T(8,128)(2,1)S(1)}, bf16[1024,512]{1,0:T(8,128)(2,1)}, u32[]{:S(2)}) copy-start(bf16[1024,512]{1,0:T(8,128)(2,1)} %get-tuple-element.83) | copy-start | bytes 3145732
  29.2 63.5 %copy-start.4 = (bf16[16,64,256]{2,1,0:T(8,128)(2,1)}, bf16[16,64,256]{2,1,0:T(8,128)(2,1)S(1)}, u32[]{:S(2)}) copy-start(bf16[16,64,256]{2,1,0:T(8,128)(2,1)S(1)} %all-to-all-done.1) | copy-start | bytes 1572868
  29.2 27.6 %all-to-all-start.3 = ((bf16[16,64,512]{2,1,0:T(8,128)(2,1)}), bf16[16,64,512]{2,1,0:T(8,128)(2,1)S(1)}, u32[]{:S(2)}, u32[]{:S(2)}) async-start(bf16[16,64,512]{2,1,0:T(8,128)(2,1)} %bitcast.16), calls=%async_computation.3 | async-start | bytes 2097152 | tf_op jit(solution)/shard_map/all_to_all | solution.py:472
  56.8 8.9 %copy-start.2 = (bf16[16,64,512]{2,1,0:T(8,128)(2,1)}, bf16[16,64,512]{2,1,0:T(8,128)(2,1)S(1)}, u32[]{:S(2)}) copy-start(bf16[16,64,512]{2,1,0:T(8,128)(2,1)S(1)} %all-to-all-done.3) | copy-start | bytes 3145732
  56.8 28.8 %all-to-all-start.2 = ((bf16[16,64,512]{2,1,0:T(8,128)(2,1)}), bf16[16,64,512]{2,1,0:T(8,128)(2,1)S(1)}, u32[]{:S(2)}, u32[]{:S(2)}) async-start(bf16[16,64,512]{2,1,0:T(8,128)(2,1)} %bitcast.30), calls=%async_computation.2 | async-start | bytes 2097152 | tf_op jit(solution)/shard_map/all_to_all | solution.py:472
  65.7 27.1 %copy-start.24 = (f32[24]{0:T(128)S(1)}, f32[24]{0:T(128)}, u32[]{:S(2)}) copy-start(f32[24]{0:T(128)} %param.19) | copy-start | bytes 292
  65.7 27.1 %copy-start.25 = (f32[24]{0:T(128)S(1)}, f32[24]{0:T(128)}, u32[]{:S(2)}) copy-start(f32[24]{0:T(128)} %param.17) | copy-start | bytes 292
  65.7 27.1 %copy-start.26 = (f32[24]{0:T(128)S(1)}, f32[24]{0:T(128)}, u32[]{:S(2)}) copy-start(f32[24]{0:T(128)} %param.18) | copy-start | bytes 292
  85.6 1.0 copy-start.3
  86.6 50.2 %all-to-all-start = ((bf16[16,64,512]{2,1,0:T(8,128)(2,1)}), bf16[16,64,512]{2,1,0:T(8,128)(2,1)S(1)}, u32[]{:S(2)}, u32[]{:S(2)}) async-start(bf16[16,64,512]{2,1,0:T(8,128)(2,1)} %bitcast.29), calls=%async_computation | async-start | bytes 2097152 | tf_op jit(solution)/shard_map/all_to_all | solution.py:472
  92.7 1.6 collective-permute-start
  94.3 0.7 copy-start.14
  108.8 12.9 %collective-permute-start.10 = (f32[2,40,1024]{2,1,0:T(8,128)}, f32[2,40,1024]{2,1,0:T(8,128)S(1)}, u32[]{:S(2)}, u32[]{:S(2)}) collective-permute-start(f32[2,40,1024]{2,1,0:T(8,128)} %get-tuple-element.120), channel_id=1, source_target_pairs={{0,2},{2,0},{4,6},{6,4},{8,10},{10,8},{12,14},{14,12},{16,18},{18,... | collective-permute-start | bytes 983048 | tf_op jit(solution)/shard_map/ppermute | solution.py:514
  110.8 10.9 %collective-permute-start.11 = (f32[2,40,1024]{2,1,0:T(8,128)}, f32[2,40,1024]{2,1,0:T(8,128)S(1)}, u32[]{:S(2)}, u32[]{:S(2)}) collective-permute-start(f32[2,40,1024]{2,1,0:T(8,128)} %get-tuple-element.121), channel_id=1, source_target_pairs={{0,4},{2,6},{4,0},{6,2},{8,12},{10,14},{12,8},{14,10},{16,20},{18,... | collective-permute-start | bytes 983048 | tf_op jit(solution)/shard_map/ppermute | solution.py:514
  112.3 16.9 %collective-permute-start.12 = (f32[2,40,1024]{2,1,0:T(8,128)}, f32[2,40,1024]{2,1,0:T(8,128)S(1)}, u32[]{:S(2)}, u32[]{:S(2)}) collective-permute-start(f32[2,40,1024]{2,1,0:T(8,128)} %get-tuple-element.122), channel_id=1, source_target_pairs={{0,6},{2,4},{4,2},{6,0},{8,14},{10,12},{12,10},{14,8},{16,22},{18,... | collective-permute-start | bytes 983048 | tf_op jit(solution)/shard_map/ppermute | solution.py:514
  121.7 7.4 %copy-start.5 = (f32[2,40,1024]{2,1,0:T(8,128)}, f32[2,40,1024]{2,1,0:T(8,128)S(1)}, u32[]{:S(2)}) copy-start(f32[2,40,1024]{2,1,0:T(8,128)S(1)} %collective-permute-done.10.p1_ref) | copy-start | bytes 983044
  121.7 7.4 %copy-start.6 = (f32[2,40,1024]{2,1,0:T(8,128)}, f32[2,40,1024]{2,1,0:T(8,128)S(1)}, u32[]{:S(2)}) copy-start(f32[2,40,1024]{2,1,0:T(8,128)S(1)} %collective-permute-done.11.p2_ref) | copy-start | bytes 983044
  129.1 0.7 copy-start.7
  132.1 12.0 %collective-permute-start.13 = (f32[40,1024]{1,0:T(8,128)}, f32[40,1024]{1,0:T(8,128)S(1)}, u32[]{:S(2)}, u32[]{:S(2)}) collective-permute-start(f32[40,1024]{1,0:T(8,128)} %get-tuple-element.123), channel_id=1, source_target_pairs={{0,8},{2,10},{4,12},{6,14},{8,0},{10,2},{12,4},{14,6},{16,24},{18,... | collective-permute-start | bytes 491528 | tf_op jit(solution)/shard_map/ppermute | solution.py:530
  134.4 15.0 %collective-permute-start.14 = (f32[40,1024]{1,0:T(8,128)}, f32[40,1024]{1,0:T(8,128)S(1)}, u32[]{:S(2)}, u32[]{:S(2)}) collective-permute-start(f32[40,1024]{1,0:T(8,128)} %get-tuple-element.124), channel_id=1, source_target_pairs={{0,16},{2,18},{4,20},{6,22},{8,24},{10,26},{12,28},{14,30},{16,0},... | collective-permute-start | bytes 491528 | tf_op jit(solution)/shard_map/ppermute | solution.py:530
  136.3 13.2 %collective-permute-start.15 = (f32[40,1024]{1,0:T(8,128)}, f32[40,1024]{1,0:T(8,128)S(1)}, u32[]{:S(2)}, u32[]{:S(2)}) collective-permute-start(f32[40,1024]{1,0:T(8,128)} %get-tuple-element.125), channel_id=1, source_target_pairs={{0,24},{2,26},{4,28},{6,30},{8,16},{10,18},{12,20},{14,22},{16,8},... | collective-permute-start | bytes 491528 | tf_op jit(solution)/shard_map/ppermute | solution.py:530
  136.8 1.0 copy-start.1
  142.1 12.4 %collective-permute-start.1 = (f32[2,40,512]{2,1,0:T(8,128)}, f32[2,40,512]{2,1,0:T(8,128)S(1)}, u32[]{:S(2)}, u32[]{:S(2)}) collective-permute-start(f32[2,40,512]{2,1,0:T(8,128)} %get-tuple-element.99), channel_id=1, source_target_pairs={{0,2},{2,0},{4,6},{6,4},{8,10},{10,8},{12,14},{14,12},{16,18},{18,... | collective-permute-start | bytes 491528 | tf_op jit(solution)/shard_map/ppermute | solution.py:514
  143.7 10.9 %collective-permute-start.2 = (f32[2,40,512]{2,1,0:T(8,128)}, f32[2,40,512]{2,1,0:T(8,128)S(1)}, u32[]{:S(2)}, u32[]{:S(2)}) collective-permute-start(f32[2,40,512]{2,1,0:T(8,128)} %get-tuple-element.100), channel_id=1, source_target_pairs={{0,4},{2,6},{4,0},{6,2},{8,12},{10,14},{12,8},{14,10},{16,20},{18,... | collective-permute-start | bytes 491528 | tf_op jit(solution)/shard_map/ppermute | solution.py:514
  144.2 5.3 %copy-start.15 = (f32[40,1024]{1,0:T(8,128)}, f32[40,1024]{1,0:T(8,128)S(1)}, u32[]{:S(2)}) copy-start(f32[40,1024]{1,0:T(8,128)S(1)} %collective-permute-done.13.refs_0_) | copy-start | bytes 491524
  144.2 10.4 %collective-permute-start.3 = (f32[2,40,512]{2,1,0:T(8,128)}, f32[2,40,512]{2,1,0:T(8,128)S(1)}, u32[]{:S(2)}, u32[]{:S(2)}) collective-permute-start(f32[2,40,512]{2,1,0:T(8,128)} %get-tuple-element.101), channel_id=1, source_target_pairs={{0,6},{2,4},{4,2},{6,0},{8,14},{10,12},{12,10},{14,8},{16,22},{18,... | collective-permute-start | bytes 491528 | tf_op jit(solution)/shard_map/ppermute | solution.py:514
  149.4 0.7 copy-start.16
  149.4 0.7 copy-start.17
  152.9 21.9 %collective-permute-start.16 = (f32[2,32,1024]{2,1,0:T(8,128)}, f32[2,32,1024]{2,1,0:T(8,128)S(1)}, u32[]{:S(2)}, u32[]{:S(2)}) collective-permute-start(f32[2,32,1024]{2,1,0:T(8,128)} %get-tuple-element.127), channel_id=1, source_target_pairs={{0,2},{2,0},{4,6},{6,4},{8,10},{10,8},{12,14},{14,12},{16,18},{18,... | collective-permute-start | bytes 786440 | tf_op jit(solution)/shard_map/ppermute | solution.py:514
  154.6 0.7 copy-start.11
  154.6 0.7 copy-start.12
  154.6 0.8 copy-start.13
  157.3 5.2 %collective-permute-start.4 = (f32[40,512]{1,0:T(8,128)}, f32[40,512]{1,0:T(8,128)S(1)}, u32[]{:S(2)}, u32[]{:S(2)}) collective-permute-start(f32[40,512]{1,0:T(8,128)} %get-tuple-element.102), channel_id=1, source_target_pairs={{0,8},{2,10},{4,12},{6,14},{8,0},{10,2},{12,4},{14,6},{16,24},{18,... | collective-permute-start | bytes 245768 | tf_op jit(solution)/shard_map/ppermute | solution.py:530
  159.9 32.8 %collective-permute-start.17 = (f32[2,32,1024]{2,1,0:T(8,128)}, f32[2,32,1024]{2,1,0:T(8,128)S(1)}, u32[]{:S(2)}, u32[]{:S(2)}) collective-permute-start(f32[2,32,1024]{2,1,0:T(8,128)} %get-tuple-element.128), channel_id=1, source_target_pairs={{0,4},{2,6},{4,0},{6,2},{8,12},{10,14},{12,8},{14,10},{16,20},{18,... | collective-permute-start | bytes 786440 | tf_op jit(solution)/shard_map/ppermute | solution.py:514
  160.4 32.3 %collective-permute-start.18 = (f32[2,32,1024]{2,1,0:T(8,128)}, f32[2,32,1024]{2,1,0:T(8,128)S(1)}, u32[]{:S(2)}, u32[]{:S(2)}) collective-permute-start(f32[2,32,1024]{2,1,0:T(8,128)} %get-tuple-element.129), channel_id=1, source_target_pairs={{0,6},{2,4},{4,2},{6,0},{8,14},{10,12},{12,10},{14,8},{16,22},{18,... | collective-permute-start | bytes 786440 | tf_op jit(solution)/shard_map/ppermute | solution.py:514
  161.5 6.4 %collective-permute-start.5 = (f32[40,512]{1,0:T(8,128)}, f32[40,512]{1,0:T(8,128)S(1)}, u32[]{:S(2)}, u32[]{:S(2)}) collective-permute-start(f32[40,512]{1,0:T(8,128)} %get-tuple-element.103), channel_id=1, source_target_pairs={{0,16},{2,18},{4,20},{6,22},{8,24},{10,26},{12,28},{14,30},{16,0},... | collective-permute-start | bytes 245768 | tf_op jit(solution)/shard_map/ppermute | solution.py:530
  162.5 6.6 %copy-start.21 = (f32[40,512]{1,0:T(8,128)}, f32[40,512]{1,0:T(8,128)S(1)}, u32[]{:S(2)}) copy-start(f32[40,512]{1,0:T(8,128)S(1)} %collective-permute-done.4.refs_0_) | copy-start | bytes 245764
  162.5 6.5 %collective-permute-start.6 = (f32[40,512]{1,0:T(8,128)}, f32[40,512]{1,0:T(8,128)S(1)}, u32[]{:S(2)}, u32[]{:S(2)}) collective-permute-start(f32[40,512]{1,0:T(8,128)} %get-tuple-element.104), channel_id=1, source_target_pairs={{0,24},{2,26},{4,28},{6,30},{8,16},{10,18},{12,20},{14,22},{16,8},... | collective-permute-start | bytes 245768 | tf_op jit(solution)/shard_map/ppermute | solution.py:530
  167.9 1.2 copy-start.22
  169.1 0.6 copy-start.23
  172.1 42.4 %collective-permute-start.7 = (f32[2,32,512]{2,1,0:T(8,128)}, f32[2,32,512]{2,1,0:T(8,128)S(1)}, u32[]{:S(2)}, u32[]{:S(2)}) collective-permute-start(f32[2,32,512]{2,1,0:T(8,128)} %get-tuple-element.106), channel_id=1, source_target_pairs={{0,2},{2,0},{4,6},{6,4},{8,10},{10,8},{12,14},{14,12},{16,18},{18,... | collective-permute-start | bytes 393224 | tf_op jit(solution)/shard_map/ppermute | solution.py:514
  174.2 40.2 %collective-permute-start.8 = (f32[2,32,512]{2,1,0:T(8,128)}, f32[2,32,512]{2,1,0:T(8,128)S(1)}, u32[]{:S(2)}, u32[]{:S(2)}) collective-permute-start(f32[2,32,512]{2,1,0:T(8,128)} %get-tuple-element.107), channel_id=1, source_target_pairs={{0,4},{2,6},{4,0},{6,2},{8,12},{10,14},{12,8},{14,10},{16,20},{18,... | collective-permute-start | bytes 393224 | tf_op jit(solution)/shard_map/ppermute | solution.py:514
  174.8 6.6 %copy-start.8 = (f32[2,32,1024]{2,1,0:T(8,128)}, f32[2,32,1024]{2,1,0:T(8,128)S(1)}, u32[]{:S(2)}) copy-start(f32[2,32,1024]{2,1,0:T(8,128)S(1)} %collective-permute-done.16.s1_ref) | copy-start | bytes 786436
  174.8 39.7 %collective-permute-start.9 = (f32[2,32,512]{2,1,0:T(8,128)}, f32[2,32,512]{2,1,0:T(8,128)S(1)}, u32[]{:S(2)}, u32[]{:S(2)}) collective-permute-start(f32[2,32,512]{2,1,0:T(8,128)} %get-tuple-element.108), channel_id=1, source_target_pairs={{0,6},{2,4},{4,2},{6,0},{8,14},{10,12},{12,10},{14,8},{16,22},{18,... | collective-permute-start | bytes 393224 | tf_op jit(solution)/shard_map/ppermute | solution.py:514
  192.7 0.7 copy-start.9
  192.7 0.8 copy-start.10
  214.4 0.6 copy-start.18
  214.4 0.7 copy-start.19
  214.5 0.7 copy-start.20
  229.2 2.1 collective-permute-start.19
